TPU v7x, 32 devices: a whole 2x2x4 slice. The times are simulated.
32 devices in a mesh: seq: 16 (over z, y, core), head: 2 (over x).
Axes of the slice: x: 2, y: 2, z: 4, core: 2. Of those that a mesh axis runs over, the one named last changes fastest.
Arguments:
- queries: bfloat16 [8192, 4096], P('seq', 'head'), may hold values from -20 to 20
- key_rows: bfloat16 [8192, 2048], P('seq', 'head'), may hold values from -20 to 20
- values: bfloat16 [8192, 2048], P('seq', 'head'), may hold values from -24 to 24
- out_weight: bfloat16 [4096, 5376], P('head'), may hold values from -0.09375 to 0.09375
Outputs:
- projected: bfloat16 [8192, 5376], P(('seq', 'head'))
All inputs are finite; a program needn't handle non-finite values.
Results may differ from a plain program's by a relative error of at most 0.019.
Values may be sent and summed in bfloat16 or wider, within the bound.
A program may use at most 192 MiB of HBM per device.

v0:
```python
import jax
import jax.numpy as jnp
from jax import lax
from jax.sharding import PartitionSpec as P

HD = 128


attn_scale = 168.0 ** (-0.5)
neg_fill = -1e30
key_block = 512


def from_behind(value, axis, steps):
    count = lax.axis_size(axis)
    leading, last = (max(0, -steps), min(count, count - steps))
    return lax.ppermute(value, axis, [(source, source + steps) for source in range(leading, last)])


def for_sending(x):

    def short(part):
        return part.astype(jnp.bfloat16) if part.dtype == jnp.float32 else part

    return jax.tree.map(short, x)


def attend(states, query_part, query_begin, key_part, value_part, key_begin, key_low, key_high):
    query_len = query_part.shape[0]
    key_len = key_part.shape[0]
    needed = (
        (key_begin <= query_begin + query_len - 1)
        & (key_begin + key_len > key_low)
        & (key_begin < key_high)
    )

    def compute(states):
        row_max, row_sum, summed = states
        query_pos = query_begin + jnp.arange(query_len, dtype=jnp.int32)
        key_pos = key_begin + jnp.arange(key_len, dtype=jnp.int32)
        allowed = (
            (key_pos[None, :] <= query_pos[:, None])
            & (key_pos[None, :] >= key_low)
            & (key_pos[None, :] < key_high)
        )
        scores = (
            jnp.einsum("qhgd,khd->hgqk", query_part, key_part, preferred_element_type=jnp.float32)
            * attn_scale
        )
        scores = jnp.where(allowed[None, None], scores, neg_fill)
        new_max = jnp.maximum(row_max, jnp.max(scores, axis=-1))
        weights = jnp.where(allowed[None, None], jnp.exp(scores - new_max[..., None]), 0.0)
        factor = jnp.exp(row_max - new_max)
        new_sum = row_sum * factor + jnp.sum(weights, axis=-1)
        rounded = weights.astype(jnp.bfloat16)
        new_summed = summed * factor[..., None] + jnp.einsum(
            "hgqk,khd->hgqd", rounded, value_part, preferred_element_type=jnp.float32
        )
        return (new_max, new_sum, new_summed)

    return lax.cond(needed, compute, lambda kept: kept, states)


def fresh_state(value_heads, per_group, local_rows):
    return (
        jnp.full((value_heads, per_group, local_rows), neg_fill, jnp.float32),
        jnp.zeros((value_heads, per_group, local_rows), jnp.float32),
        jnp.zeros((value_heads, per_group, local_rows, HD), jnp.float32),
    )


def per_device(queries, key_rows, values, out_weight):
    spans = lax.axis_size("seq")
    myself = lax.axis_index("seq")
    local_rows = queries.shape[0]
    value_heads = key_rows.shape[1] // HD
    query_heads = queries.shape[1] // HD
    per_group = query_heads // value_heads
    own_grid = queries.reshape(local_rows, value_heads, per_group, HD)
    own_begin = myself * local_rows
    query_sets = []
    half_axis = spans // 2
    lent_limit = spans // 4 * local_rows
    is_late = myself >= half_axis
    own_low = jnp.where(is_late, lent_limit, 0).astype(jnp.int32)
    query_sets.append((own_grid, own_begin, own_low, jnp.int32(2**30)))
    lent = from_behind(queries, "seq", -half_axis)
    lent_grid = lent.reshape(local_rows, value_heads, per_group, HD)
    lent_high = jnp.where(is_late, 0, lent_limit).astype(jnp.int32)
    query_sets.append((lent_grid, (myself + half_axis) * local_rows, jnp.int32(0), lent_high))
    initial = tuple((fresh_state(value_heads, per_group, local_rows) for entry in query_sets))
    key_piece = lax.all_gather(key_rows, "seq", axis=0, tiled=True)
    value_piece = lax.all_gather(values, "seq", axis=0, tiled=True)
    piece_rows = key_piece.shape[0]
    block_total = piece_rows // key_block

    def advance(block_id, inner):
        key_slab = lax.dynamic_slice_in_dim(key_piece, block_id * key_block, key_block, 0).reshape(
            key_block, value_heads, HD
        )
        value_slab = lax.dynamic_slice_in_dim(
            value_piece, block_id * key_block, key_block, 0
        ).reshape(key_block, value_heads, HD)
        key_begin = block_id * key_block
        return tuple(
            (
                attend(state_one, grid, begin, key_slab, value_slab, key_begin, lower, upper)
                for state_one, (grid, begin, lower, upper) in zip(inner, query_sets)
            )
        )

    results = lax.fori_loop(0, block_total, advance, initial)
    row_max, row_sum, summed = results[0]
    back_max, back_sum, back_summed = from_behind(for_sending(results[1]), "seq", spans // 2)
    back_max = jnp.where(myself >= spans // 2, back_max, neg_fill)
    joint_max = jnp.maximum(row_max, back_max)
    own_factor = jnp.exp(row_max - joint_max)
    back_factor = jnp.exp(back_max - joint_max)
    row_sum = row_sum * own_factor + back_sum * back_factor
    summed = summed * own_factor[..., None] + back_summed * back_factor[..., None]
    attended = (
        (summed / row_sum[..., None])
        .transpose(2, 0, 1, 3)
        .reshape(local_rows, query_heads * HD)
        .astype(jnp.bfloat16)
    )
    return lax.psum_scatter(
        jnp.dot(attended, out_weight, preferred_element_type=jnp.float32).astype(jnp.bfloat16),
        "head",
        scatter_dimension=0,
        tiled=True,
    )


def solution(mesh):
    placed = (P("seq", "head"), P("seq", "head"), P("seq", "head"), P("head", None))
    return jax.shard_map(
        per_device, mesh=mesh, in_specs=placed, out_specs=P(("seq", "head"), None), check_vma=False
    )
```

profile of v0, /device:TPU:0, one launch (start us, length us, event | category | flops | bytes accessed | tf_op | source)
XLA Modules:
  0.0 802.0 jit_solution(6045147930715456967)
XLA Ops:
  6.5 2.3 copy.13
  8.9 2.3 copy.14
  11.3 3.9 copy.15
  16.5 3.1 copy.17
  19.6 179.8 %collective-permute-done = bf16[512,2048]{0,1:T(8,128)(2,1)} collective-permute-done((bf16[512,2048]{0,1:T(8,128)(2,1)}, bf16[512,2048]{0,1:T(8,128)(2,1)}, u32[]{:S(2)}, u32[]{:S(2)}) %collective-permute-start) | collective-permute-done | bytes 2097184 | tf_op jit(solution)/shard_map/ppermute | solution.py:17
  199.4 3.9 copy.18
  203.3 14.5 %all-gather.3.cloned.1.call-done = bf16[8192,1024]{0,1:T(8,128)(2,1)} async-done(((bf16[512,1024]{0,1:T(8,128)(2,1)}), bf16[8192,1024]{0,1:T(8,128)(2,1)}) %all-gather.3.cloned.1.call-update) | async-done | bytes 16777232 | tf_op jit(solution)/shard_map/all_gather | solution.py:92
  217.8 133.6 %all-gather.5.cloned.1.call-done = bf16[8192,1024]{0,1:T(8,128)(2,1)} async-done(((bf16[512,1024]{0,1:T(8,128)(2,1)}), bf16[8192,1024]{0,1:T(8,128)(2,1)}) %all-gather.5.cloned.1.call-update) | async-done | bytes 16777232 | tf_op jit(solution)/shard_map/all_gather | solution.py:93
  351.5 2.4 broadcast.162.clone
  353.9 2.5 broadcast.162
  356.4 161.2 %while.26 = (s32[]{:T(128)}, f32[8,2,512]{2,1,0:T(2,128)S(1)}, f32[8,2,512]{2,1,0:T(2,128)S(1)}, f32[8,2,512,128]{3,2,1,0:T(8,128)}, f32[8,2,512]{2,1,0:T(2,128)...) while((s32[]{:T(128)}, f32[8,2,512]{2,1,0:T(2,128)S(1)}, ...), condition=%wide.region_9.10_spmd, body=%wide.region_0.9_spmd.sunk | while | flops 4409824256 | bytes 342905664 | solution.py:112
  356.4 2.7 constant_dynamic-slice_fusion.3
  359.1 22.8 %conditional.4 = ((f32[8,2,512]{2,1,0:T(2,128)S(1)}, f32[8,2,512]{2,1,0:T(2,128)S(1)}, f32[8,2,512,128]{3,2,1,0:T(8,128)})) conditional(s32[]{:T(128)} %convert_element_type.91, (f32[8,2,512]{2,1,0:T(2,128)S(1)}, f32[8,2,512]{2,1,0:T(2,128)S(1)}, f32[8,2,512,128]{3,2,1,0:T(8,128)}) %tuple.74, (s32[]{:T(128)}, s32[]{:T(128)}, s32[]{:T(128)}, ...), branch_computations={%region_1.1_spmd, %region_2.4_spmd} | conditional | flops 2204912128 | bytes 169355424 | solution.py:61
  359.4 3.8 fusion
  363.2 4.0 fusion.2
  367.2 3.3 copy-done
  370.6 9.2 %multiply_add_fusion = f32[8,2,512,128]{3,2,1,0:T(8,128)S(1)} fusion(f32[8,2,512,128]{3,2,1,0:T(8,128)S(1)} %copy-done.6, f32[8,2,512]{2,1,0:T(2,128)S(1)} %bitcast.92, f32[8,512,512,2]{2,1,3,0:T(8,128)} %copy-done, f32[8,2,512]{2,1,0:T(2,128)S(1)} %max.6, pred[512,512]{0,1:T(8,128)(4,1)S(1)} %and_and_fusion, bf16[512,8,128]{0,2,1:T(8,128)(2,1)S(1)} %copy-done.2), kind=kOutput, calls=%fused_computation.7 | convolution fusion | flops 1096810496 | bytes 26542080 | tf_op jit(solution)/shard_map/while/body/eval_jaxpr/cond/branch_1_fun/hgqk,khd->hgqd/dot_general | solution.py:56
  379.8 2.1 copy-done.7
  381.9 24.0 %conditional.5 = ((f32[8,2,512]{2,1,0:T(2,128)S(1)}, f32[8,2,512]{2,1,0:T(2,128)S(1)}, f32[8,2,512,128]{3,2,1,0:T(8,128)})) conditional(s32[]{:T(128)} %convert_element_type.92, (f32[8,2,512]{2,1,0:T(2,128)S(1)}, f32[8,2,512]{2,1,0:T(2,128)S(1)}, f32[8,2,512,128]{3,2,1,0:T(8,128)}) %tuple.76, (s32[]{:T(128)}, s32[]{:T(128)}, s32[]{:T(128)}, ...), branch_computations={%region_5.5_spmd, %region_6.8_spmd} | conditional | flops 2204912128 | bytes 169355424 | solution.py:61
  382.2 5.0 fusion.16
  387.2 4.0 fusion.18
  391.3 3.3 copy-done.1
  394.7 9.2 %multiply_add_fusion.2 = f32[8,2,512,128]{3,2,1,0:T(8,128)S(1)} fusion(f32[8,2,512,128]{3,2,1,0:T(8,128)S(1)} %copy-done.4, f32[8,2,512]{2,1,0:T(2,128)S(1)} %bitcast.93, f32[8,512,512,2]{2,1,3,0:T(8,128)} %copy-done.1, f32[8,2,512]{2,1,0:T(2,128)S(1)} %max.7, pred[512,512]{0,1:T(8,128)(4,1)S(1)} %and_and_fusion.1, bf16[512,8,128]{0,2,1:T(8,128)(2,1)S(1)} %copy-done.3), kind=kOutput, calls=%fused_computation.28 | convolution fusion | flops 1096810496 | bytes 26542080 | tf_op jit(solution)/shard_map/while/body/eval_jaxpr/cond/branch_1_fun/hgqk,khd->hgqd/dot_general | solution.py:56
  403.8 2.0 copy-done.5
  405.8 2.7 constant_dynamic-slice_fusion.3
  408.5 24.0 %conditional.5 = ((f32[8,2,512]{2,1,0:T(2,128)S(1)}, f32[8,2,512]{2,1,0:T(2,128)S(1)}, f32[8,2,512,128]{3,2,1,0:T(8,128)})) conditional(s32[]{:T(128)} %convert_element_type.92, (f32[8,2,512]{2,1,0:T(2,128)S(1)}, f32[8,2,512]{2,1,0:T(2,128)S(1)}, f32[8,2,512,128]{3,2,1,0:T(8,128)}) %tuple.76, (s32[]{:T(128)}, s32[]{:T(128)}, s32[]{:T(128)}, ...), branch_computations={%region_5.5_spmd, %region_6.8_spmd} | conditional | flops 2204912128 | bytes 169355424 | solution.py:61
  408.8 5.0 fusion.16
  413.9 4.0 fusion.18
  417.9 3.3 copy-done.1
  421.3 9.2 %multiply_add_fusion.2 = f32[8,2,512,128]{3,2,1,0:T(8,128)S(1)} fusion(f32[8,2,512,128]{3,2,1,0:T(8,128)S(1)} %copy-done.4, f32[8,2,512]{2,1,0:T(2,128)S(1)} %bitcast.93, f32[8,512,512,2]{2,1,3,0:T(8,128)} %copy-done.1, f32[8,2,512]{2,1,0:T(2,128)S(1)} %max.7, pred[512,512]{0,1:T(8,128)(4,1)S(1)} %and_and_fusion.1, bf16[512,8,128]{0,2,1:T(8,128)(2,1)S(1)} %copy-done.3), kind=kOutput, calls=%fused_computation.28 | convolution fusion | flops 1096810496 | bytes 26542080 | tf_op jit(solution)/shard_map/while/body/eval_jaxpr/cond/branch_1_fun/hgqk,khd->hgqd/dot_general | solution.py:56
  430.5 2.0 copy-done.5
  432.5 2.7 constant_dynamic-slice_fusion.3
  435.1 24.0 %conditional.5 = ((f32[8,2,512]{2,1,0:T(2,128)S(1)}, f32[8,2,512]{2,1,0:T(2,128)S(1)}, f32[8,2,512,128]{3,2,1,0:T(8,128)})) conditional(s32[]{:T(128)} %convert_element_type.92, (f32[8,2,512]{2,1,0:T(2,128)S(1)}, f32[8,2,512]{2,1,0:T(2,128)S(1)}, f32[8,2,512,128]{3,2,1,0:T(8,128)}) %tuple.76, (s32[]{:T(128)}, s32[]{:T(128)}, s32[]{:T(128)}, ...), branch_computations={%region_5.5_spmd, %region_6.8_spmd} | conditional | flops 2204912128 | bytes 169355424 | solution.py:61
  435.4 5.0 fusion.16
  440.5 4.0 fusion.18
  444.5 3.3 copy-done.1
  447.9 9.2 %multiply_add_fusion.2 = f32[8,2,512,128]{3,2,1,0:T(8,128)S(1)} fusion(f32[8,2,512,128]{3,2,1,0:T(8,128)S(1)} %copy-done.4, f32[8,2,512]{2,1,0:T(2,128)S(1)} %bitcast.93, f32[8,512,512,2]{2,1,3,0:T(8,128)} %copy-done.1, f32[8,2,512]{2,1,0:T(2,128)S(1)} %max.7, pred[512,512]{0,1:T(8,128)(4,1)S(1)} %and_and_fusion.1, bf16[512,8,128]{0,2,1:T(8,128)(2,1)S(1)} %copy-done.3), kind=kOutput, calls=%fused_computation.28 | convolution fusion | flops 1096810496 | bytes 26542080 | tf_op jit(solution)/shard_map/while/body/eval_jaxpr/cond/branch_1_fun/hgqk,khd->hgqd/dot_general | solution.py:56
  457.1 2.0 copy-done.5
  459.1 2.7 constant_dynamic-slice_fusion.3
  461.8 24.0 %conditional.5 = ((f32[8,2,512]{2,1,0:T(2,128)S(1)}, f32[8,2,512]{2,1,0:T(2,128)S(1)}, f32[8,2,512,128]{3,2,1,0:T(8,128)})) conditional(s32[]{:T(128)} %convert_element_type.92, (f32[8,2,512]{2,1,0:T(2,128)S(1)}, f32[8,2,512]{2,1,0:T(2,128)S(1)}, f32[8,2,512,128]{3,2,1,0:T(8,128)}) %tuple.76, (s32[]{:T(128)}, s32[]{:T(128)}, s32[]{:T(128)}, ...), branch_computations={%region_5.5_spmd, %region_6.8_spmd} | conditional | flops 2204912128 | bytes 169355424 | solution.py:61
  462.1 5.0 fusion.16
  467.1 4.0 fusion.18
  471.2 3.3 copy-done.1
  474.6 9.2 %multiply_add_fusion.2 = f32[8,2,512,128]{3,2,1,0:T(8,128)S(1)} fusion(f32[8,2,512,128]{3,2,1,0:T(8,128)S(1)} %copy-done.4, f32[8,2,512]{2,1,0:T(2,128)S(1)} %bitcast.93, f32[8,512,512,2]{2,1,3,0:T(8,128)} %copy-done.1, f32[8,2,512]{2,1,0:T(2,128)S(1)} %max.7, pred[512,512]{0,1:T(8,128)(4,1)S(1)} %and_and_fusion.1, bf16[512,8,128]{0,2,1:T(8,128)(2,1)S(1)} %copy-done.3), kind=kOutput, calls=%fused_computation.28 | convolution fusion | flops 1096810496 | bytes 26542080 | tf_op jit(solution)/shard_map/while/body/eval_jaxpr/cond/branch_1_fun/hgqk,khd->hgqd/dot_general | solution.py:56
  483.7 2.0 copy-done.5
  485.7 2.7 constant_dynamic-slice_fusion.3
  488.4 2.7 constant_dynamic-slice_fusion.3
  491.0 2.7 constant_dynamic-slice_fusion.3
  493.7 2.7 constant_dynamic-slice_fusion.3
  496.4 2.7 constant_dynamic-slice_fusion.3
  499.0 2.7 constant_dynamic-slice_fusion.3
  501.7 2.7 constant_dynamic-slice_fusion.3
  504.3 2.7 constant_dynamic-slice_fusion.3
  507.0 2.7 constant_dynamic-slice_fusion.3
  509.6 2.7 constant_dynamic-slice_fusion.3
  512.3 2.7 constant_dynamic-slice_fusion.3
  515.0 2.7 constant_dynamic-slice_fusion.3
  517.6 3.3 copy.20
  521.0 2.6 collective-permute-start.2
  526.4 5.3 copy.19
  531.8 14.5 %collective-permute-done.3 = bf16[8,2,512]{2,1,0:T(2,128)(2,1)S(1)} collective-permute-done((bf16[8,2,512]{2,1,0:T(2,128)(2,1)S(1)}, bf16[8,2,512]{2,1,0:T(2,128)(2,1)S(1)}, u32[]{:S(2)}, u32[]{:S(2)}) %collective-permute-start.3) | collective-permute-done | bytes 16416 | tf_op jit(solution)/shard_map/ppermute | solution.py:17
  546.7 3.7 divide_convert_fusion
  550.5 18.6 %convolution_convert_fusion = bf16[512,5376]{1,0:T(8,128)(2,1)} fusion(bf16[512,2048]{0,1:T(8,128)(2,1)S(1)} %bitcast.87, bf16[2048,5376]{1,0:T(8,128)(2,1)} %param.13), kind=kOutput, calls=%fused_computation.44 | convolution fusion | flops 11277041664 | bytes 29622272 | tf_op jit(solution)/shard_map/dot_general | solution.py:128
  569.0 226.5 %reduce-scatter.2.cloned.1.call-done = bf16[256,5376]{1,0:T(8,128)(2,1)} async-done(((bf16[512,5376]{1,0:T(8,128)(2,1)}), bf16[256,5376]{1,0:T(8,128)(2,1)}) %reduce-scatter.2.cloned.1.call-update) | async-done | bytes 2752528 | tf_op jit(solution)/shard_map/reduce_scatter | solution.py:127
  (105 shorter events, 6.4 us)
Async XLA Ops:
  6.5 211.2 %all-gather.3.cloned.1.call-start = ((), (), s32[]{:S(2)}) async-start(), calls=%async_computation.1 | async-start | bytes 17825792 | tf_op jit(solution)/shard_map/all_gather | solution.py:92
  8.8 342.5 %all-gather.5.cloned.1.call-start = ((), (), s32[]{:S(2)}) async-start(), calls=%async_computation.2 | async-start | bytes 17825792 | tf_op jit(solution)/shard_map/all_gather | solution.py:93
  11.2 784.3 %reduce-scatter.2.cloned.1.call-start = ((), (), s32[]{:S(2)}) async-start(), calls=%async_computation.3 | async-start | bytes 8257536 | tf_op jit(solution)/shard_map/reduce_scatter | solution.py:127
  15.2 184.2 %collective-permute-start = (bf16[512,2048]{0,1:T(8,128)(2,1)}, bf16[512,2048]{0,1:T(8,128)(2,1)}, u32[]{:S(2)}, u32[]{:S(2)}) collective-permute-start(bf16[512,2048]{0,1:T(8,128)(2,1)} %copy.15), channel_id=1, source_target_pairs={{16,0},{18,2},{20,4},{22,6},{24,8},{26,10},{28,12},{30,14},{17,1},... | collective-permute-start | bytes 6291464 | tf_op jit(solution)/shard_map/ppermute | solution.py:17
  363.1 7.4 copy-start
  363.2 7.4 copy-start.2
  363.2 7.4 copy-start.6
  379.8 2.1 copy-start.7
  387.2 7.4 copy-start.1
  387.2 7.4 copy-start.3
  387.2 7.4 copy-start.4
  403.8 2.0 copy-start.5
  413.8 7.4 copy-start.1
  413.8 7.4 copy-start.3
  413.8 7.4 copy-start.4
  430.5 2.0 copy-start.5
  440.4 7.4 copy-start.1
  440.5 7.4 copy-start.3
  440.5 7.4 copy-start.4
  457.1 2.0 copy-start.5
  467.1 7.4 copy-start.1
  467.1 7.4 copy-start.3
  467.1 7.4 copy-start.4
  483.7 2.0 copy-start.5
  521.0 25.7 %collective-permute-start.2 = (bf16[8,2,512,128]{2,3,1,0:T(8,128)(2,1)S(1)}, bf16[8,2,512,128]{2,3,1,0:T(8,128)(2,1)}, u32[]{:S(2)}, u32[]{:S(2)}) collective-permute-start(bf16[8,2,512,128]{2,3,1,0:T(8,128)(2,1)S(1)} %copy.20), channel_id=1, source_target_pairs={{0,16},{2,18},{4,20},{6,22},{8,24},{10,26},{12,28},{14,30},{1,17},... | collective-permute-start | bytes 6291464 | tf_op jit(solution)/shard_map/ppermute | solution.py:17
  523.6 22.6 %collective-permute-start.3 = (bf16[8,2,512]{2,1,0:T(2,128)(2,1)S(1)}, bf16[8,2,512]{2,1,0:T(2,128)(2,1)S(1)}, u32[]{:S(2)}, u32[]{:S(2)}) collective-permute-start(bf16[8,2,512]{2,1,0:T(2,128)(2,1)S(1)} %convert_element_type.63), channel_id=1, source_target_pairs={{0,16},{2,18},{4,20},{6,22},{8,24},{10,26},{12,28},{14,30},{1,17},... | collective-permute-start | bytes 49160 | tf_op jit(solution)/shard_map/ppermute | solution.py:17
  525.1 21.5 %collective-permute-start.1 = (bf16[8,2,512]{2,1,0:T(2,128)(2,1)S(1)}, bf16[8,2,512]{2,1,0:T(2,128)(2,1)S(1)}, u32[]{:S(2)}, u32[]{:S(2)}) collective-permute-start(bf16[8,2,512]{2,1,0:T(2,128)(2,1)S(1)} %convert_element_type.59), channel_id=1, source_target_pairs={{0,16},{2,18},{4,20},{6,22},{8,24},{10,26},{12,28},{14,30},{1,17},... | collective-permute-start | bytes 49160 | tf_op jit(solution)/shard_map/ppermute | solution.py:17
Sparse Core Ops, SparseCore 0:
  9.5 208.2 all-gather.2
  219.9 131.4 all-gather.4
  569.1 226.2 reduce-scatter.1
where the time goes:
time: 804 us; the launch traced here: 802 us
  waiting for transfers between devices  569 us (71%)
  local copies, waits for them, and re-layouts  98.4 us (12%)
  matrix products  88.1 us (11%)
  other arithmetic  25.7 us (3%)
  between operations  13.2 us (2%)
    reduce_scatter x1, waiting for transfers between devices, per_device(): lax.psum_scatter(jnp.dot(attended, out_weight, preferred_element_type=jnp...  226 us
    ppermute x4, waiting for transfers between devices, from_behind(): lax.ppermute(value, axis, [(source, source + steps) for source in range(l...  195 us
    all_gather x1, waiting for transfers between devices, per_device(): value_piece = lax.all_gather(values, 'seq', axis=0, tiled=True)  134 us
    dot_general x5, matrix products, compute(): jnp.einsum('hgqk,khd->hgqd', rounded, value_part, preferred_element_type=...  45.8 us
    dynamic_slice x16, local copies, waits for them, and re-layouts, advance(): lax.dynamic_slice_in_dim(value_piece, block_id * key_block, key_block, 0)  42.5 us
    cond x45, local copies, waits for them, and re-layouts  26.8 us
    dot_general x5, matrix products, compute(): jnp.einsum('qhgd,khd->hgqk', query_part, key_part, preferred_element_type...  23.7 us
    reduce_sum x5, other arithmetic, compute(): new_sum = row_sum * factor + jnp.sum(weights, axis=-1)  20.2 us
  transfers between devices with their start and end apart: 7, of which 6 were waited for; matrix products, arithmetic and copies ran while one was open for 2% of the time, Pallas kernels for 0%

commit v1 on v0

v1 whole, which is shorter than its diff:
```python
import functools
import math

import jax
import jax.numpy as jnp
from jax import lax
from jax.experimental import pallas as pl
from jax.experimental.pallas import tpu as pltpu
from jax.sharding import PartitionSpec as P

HD = 128
SCALE = 168.0 ** (-0.5) * math.log2(math.e)
NEG = -1e30


def attn_kernel(span, width, parts, bq, bkv, q_ref, k_ref, v_ref, o_ref, kt, v1, m_s, acc_s):
    i = pl.program_id(0)
    total = k_ref.shape[0]
    pieces = 4
    step = bq // pieces
    sub = lax.rem(lax.axis_index("seq"), parts)

    @pl.when(i == 0)
    def _():
        @pl.loop(0, total // bkv)
        def _(b):
            rows = pl.ds(pl.multiple_of(b * bkv, bkv), bkv)
            flipped = k_ref[rows, :].T
            kt[:HD, rows] = flipped
            kt[HD:, rows] = flipped
            v1[rows, :HD] = v_ref[rows, :]
            v1[rows, HD:] = jnp.ones((bkv, HD), jnp.bfloat16)

    qf = q_ref[...].astype(jnp.float32) * SCALE
    high = qf.astype(jnp.bfloat16)
    low = (qf - high.astype(jnp.float32)).astype(jnp.bfloat16)
    q2 = jnp.concatenate([high, low], axis=1)
    m_s[...] = jnp.full_like(m_s, NEG)
    acc_s[...] = jnp.zeros_like(acc_s)

    def block(j, masked):
        cols = pl.ds(pl.multiple_of(j * bkv, bkv), bkv)
        for t in range(pieces):
            rows = slice(t * step, (t + 1) * step)
            s = jnp.dot(q2[rows], kt[:, cols], preferred_element_type=jnp.float32)
            if masked:
                row = i * bq + t * step + lax.broadcasted_iota(jnp.int32, (step, 1), 0)
                pos = (row // width) * span + sub * width + row % width
                col = j * bkv + lax.broadcasted_iota(jnp.int32, (1, bkv), 1)
                s = jnp.where(col <= pos, s, NEG)
            m0 = m_s[rows, :]
            m1 = jnp.maximum(m0, jnp.max(s, axis=1, keepdims=True))
            m_s[rows, :] = m1
            p = jnp.exp2(s - jnp.tile(m1, (1, bkv // HD))).astype(jnp.bfloat16)
            f = jnp.exp2(m0 - m1)
            acc_s[rows, :] = acc_s[rows, :] * jnp.tile(f, (1, 2)) + jnp.dot(
                p, v1[cols, :], preferred_element_type=jnp.float32
            )

    full = ((i * bq // width) * span + sub * width + 1) // bkv
    last = (((i + 1) * bq // width - 1) * span + sub * width + width - 1) // bkv + 1

    def one(masked, j, c):
        block(j, masked)
        return c

    lax.fori_loop(0, full, functools.partial(one, False), 0)
    lax.fori_loop(full, last, functools.partial(one, True), 0)
    a = acc_s[...]
    o_ref[...] = (a[:, :HD] / a[:, HD:]).astype(o_ref.dtype)


def attention(q, k, v, span, width, parts):
    rows, total = q.shape[0], k.shape[0]
    bq = math.gcd(rows, 1024)
    bkv = math.gcd(total, 1024)
    return pl.pallas_call(
        functools.partial(attn_kernel, span, width, parts, bq, bkv),
        grid=(rows // bq,),
        in_specs=[
            pl.BlockSpec((bq, HD), lambda i: (i, 0)),
            pl.BlockSpec((total, HD), lambda i: (0, 0)),
            pl.BlockSpec((total, HD), lambda i: (0, 0)),
        ],
        out_specs=pl.BlockSpec((bq, HD), lambda i: (i, 0)),
        out_shape=jax.ShapeDtypeStruct((rows, HD), jnp.bfloat16),
        scratch_shapes=[
            pltpu.VMEM((2 * HD, total), jnp.bfloat16),
            pltpu.VMEM((total, 2 * HD), jnp.bfloat16),
            pltpu.VMEM((bq, HD), jnp.float32),
            pltpu.VMEM((bq, 2 * HD), jnp.float32),
        ],
        compiler_params=pltpu.CompilerParams(vmem_limit_bytes=60 * 2**20),
    )(q, k, v)


def per_device(queries, key_rows, values, out_weight):
    n = lax.axis_size("seq")
    heads = lax.axis_size("head")
    mine = lax.axis_index("head")
    span = queries.shape[0]
    qh = queries.shape[1] // HD
    kvh = key_rows.shape[1] // HD
    parts = n // qh
    width = span // parts
    q = queries.reshape(parts, width, qh, HD).transpose(2, 0, 1, 3).reshape(n, width, HD)

    def spread(x):
        x = x.reshape(span, kvh, HD).transpose(1, 0, 2)
        x = jnp.repeat(x, n // kvh, axis=0)
        return lax.all_to_all(x, "seq", 0, 0, tiled=True).reshape(n * span, HD)

    q = lax.all_to_all(q, "seq", 0, 0, tiled=True).reshape(n * width, HD)
    out = attention(q, spread(key_rows), spread(values), span, width, parts)
    out = lax.all_to_all(out.reshape(n, width, HD), "seq", 0, 0, tiled=True)
    attended = out.reshape(qh, parts, width, HD).transpose(1, 2, 0, 3).reshape(span, qh * HD)
    return lax.psum_scatter(
        jnp.dot(attended, out_weight, preferred_element_type=jnp.float32).astype(jnp.bfloat16),
        "head",
        scatter_dimension=0,
        tiled=True,
    )


def solution(mesh):
    placed = (P("seq", "head"), P("seq", "head"), P("seq", "head"), P("head", None))
    return jax.shard_map(
        per_device, mesh=mesh, in_specs=placed, out_specs=P(("seq", "head"), None), check_vma=False
    )
```

time: 804 us -> 392 us (0.49)
  waiting for transfers between devices: 569 us -> 148 us
  blocking collectives: 0 us -> 110 us
  local copies, waits for them, and re-layouts: 98.4 us -> 11.4 us
  Pallas kernels: 0 us -> 70.8 us
  matrix products: 88.1 us -> 18.4 us
  other arithmetic: 25.7 us -> 0 us
  starting transfers between devices: 6.77 us -> 18.9 us
    ppermute x4 -> x0, waiting for transfers between devices: 195 us -> none  [from_behind(): lax.ppermute(value, axis, [(source, source + steps) for source in range(l...]
    reduce_scatter x1, waiting for transfers between devices: 226 us -> 69.2 us  [per_device(): lax.psum_scatter(jnp.dot(attended, out_weight, preferred_element_type=jnp...]
    all_gather x2 -> x0, waiting for transfers between devices: 148 us -> none  [the longest x1 134 us: per_device(): value_piece = lax.all_gather(values, 'seq', axis=0, tiled=True)]
    all_to_all x0 -> x2, blocking collectives: none -> 110 us  [the longest x1 58.3 us: per_device(): q = lax.all_to_all(q, 'seq', 0, 0, tiled=True).reshape(n * width, HD)]
    all_to_all x0 -> x2, waiting for transfers between devices: none -> 78.8 us  [spread(): return lax.all_to_all(x, 'seq', 0, 0, tiled=True).reshape(n * span, HD)]
    pallas_call x0 -> x1, Pallas kernels: none -> 70.8 us  [attention(): pl.pallas_call(functools.partial(attn_kernel, span, width, parts, bq, bkv...]
    dot_general x10 -> x0, matrix products: 69.6 us -> none  [the longest x5 45.8 us: compute(): jnp.einsum('hgqk,khd->hgqd', rounded, value_part, preferred_element_type=...]
    dynamic_slice x16 -> x0, local copies, waits for them, and re-layouts: 42.5 us -> none  [advance(): lax.dynamic_slice_in_dim(value_piece, block_id * key_block, key_block, 0)]
  transfers between devices with their start and end apart: 7 -> 3, of which waited for: 6 -> 3; matrix products, arithmetic and copies ran while one was open for 2% -> 1% of each run, Pallas kernels for 0% -> 0%
where the time goes in v1:
time: 392 us; the launch traced here: 391 us
  waiting for transfers between devices  148 us (38%)
  blocking collectives  110 us (28%)
  Pallas kernels  70.8 us (18%)
  starting transfers between devices  18.9 us (5%)
  matrix products  18.4 us (5%)
  between operations  13.5 us (3%)
  local copies, waits for them, and re-layouts  11.4 us (3%)
    all_to_all x2, waiting for transfers between devices, spread(): return lax.all_to_all(x, 'seq', 0, 0, tiled=True).reshape(n * span, HD)  78.8 us
    pallas_call x1, Pallas kernels, attention(): pl.pallas_call(functools.partial(attn_kernel, span, width, parts, bq, bkv...  70.8 us
    reduce_scatter x1, waiting for transfers between devices, per_device(): lax.psum_scatter(jnp.dot(attended, out_weight, preferred_element_type=jnp...  69.2 us
    all_to_all x1, blocking collectives, per_device(): q = lax.all_to_all(q, 'seq', 0, 0, tiled=True).reshape(n * width, HD)  58.3 us
    all_to_all x1, blocking collectives, per_device(): out = lax.all_to_all(out.reshape(n, width, HD), 'seq', 0, 0, tiled=True)  52.1 us
    all_to_all x2, starting transfers between devices, spread(): return lax.all_to_all(x, 'seq', 0, 0, tiled=True).reshape(n * span, HD)  18.8 us
    dot_general x1, matrix products, per_device(): jnp.dot(attended, out_weight, preferred_element_type=jnp.float32)  18.4 us
  transfers between devices with their start and end apart: 3, of which 3 were waited for; matrix products, arithmetic and copies ran while one was open for 1% of the time, Pallas kernels for 0%

profile of v1, /device:TPU:0, one launch (start us, length us, event | category | flops | bytes accessed | tf_op | source)
XLA Modules:
  0.0 391.3 jit_solution(15799949204980160410)
XLA Ops:
  6.5 1.5 copy.13
  8.0 0.1 copy.9
  8.2 1.7 broadcast_in_dim.6
  9.9 0.0 copy-start.1
  9.9 7.5 %all-to-all-start.1 = ((bf16[16,512,128]{2,1,0:T(8,128)(2,1)}), bf16[16,512,128]{2,1,0:T(8,128)(2,1)S(1)}, u32[]{:S(2)}, u32[]{:S(2)}) async-start(bf16[16,512,128]{2,1,0:T(8,128)(2,1)} %bitcast.4), calls=%async_computation.1 | async-start | bytes 4194304 | tf_op jit(solution)/shard_map/all_to_all | solution.py:111
  17.5 0.0 copy-done.1
  17.5 0.3 copy.14
  17.7 0.1 copy.10
  17.9 40.5 %all-to-all-done.1 = bf16[16,512,128]{2,1,0:T(8,128)(2,1)S(1)} async-done(((bf16[16,512,128]{2,1,0:T(8,128)(2,1)}), bf16[16,512,128]{2,1,0:T(8,128)(2,1)S(1)}, u32[]{:S(2)}, u32[]{:S(2)}) %all-to-all-start.1) | async-done | bytes 2097184 | tf_op jit(solution)/shard_map/all_to_all | solution.py:111
  58.4 0.0 copy-start
  58.4 2.0 broadcast_in_dim.7
  60.4 0.0 copy-done
  60.4 11.3 %all-to-all-start.2 = ((bf16[16,512,128]{2,1,0:T(8,128)(2,1)}), bf16[16,512,128]{2,1,0:T(8,128)(2,1)}, u32[]{:S(2)}, u32[]{:S(2)}) async-start(bf16[16,512,128]{2,1,0:T(8,128)(2,1)} %bitcast.7), calls=%async_computation.2 | async-start | bytes 4194304 | tf_op jit(solution)/shard_map/all_to_all | solution.py:111
  71.7 0.0 reduce-scatter.2.cloned.1.call-start
  71.8 2.2 copy.12
  74.0 0.5 copy.16
  74.5 38.2 %all-to-all-done.2 = bf16[16,512,128]{2,1,0:T(8,128)(2,1)} async-done(((bf16[16,512,128]{2,1,0:T(8,128)(2,1)}), bf16[16,512,128]{2,1,0:T(8,128)(2,1)}, u32[]{:S(2)}, u32[]{:S(2)}) %all-to-all-start.2) | async-done | bytes 2097184 | tf_op jit(solution)/shard_map/all_to_all | solution.py:111
  112.7 58.3 %all_to_all.20 = bf16[16,512,128]{2,1,0:T(8,128)(2,1)} all-to-all(bf16[16,512,128]{2,1,0:T(8,128)(2,1)S(1)} %bitcast.29), channel_id=1, replica_groups=mesh['seq'=16,'head'=2] {'seq'}, dimensions={0} | all-to-all | bytes 4194304 | tf_op jit(solution)/shard_map/all_to_all | solution.py:113
  171.0 70.8 %shard_map.46 = bf16[8192,128]{1,0:T(8,128)(2,1)} custom-call(bf16[8192,128]{1,0:T(8,128)(2,1)} %bitcast.32, bf16[8192,128]{1,0:T(8,128)(2,1)} %bitcast.31, bf16[8192,128]{1,0:T(8,128)(2,1)} %bitcast.8.v_ref), custom_call_target="tpu_custom_call" | custom-call | tf_op jit(solution)/shard_map/pallas_call | solution.py:77
  241.8 2.9 copy.11
  244.7 52.1 %all_to_all.21 = bf16[16,512,128]{1,2,0:T(8,128)(2,1)S(1)} all-to-all(bf16[16,512,128]{1,2,0:T(8,128)(2,1)S(1)} %copy.11), channel_id=1, replica_groups=mesh['seq'=16,'head'=2] {'seq'}, dimensions={0} | all-to-all | bytes 4194304 | tf_op jit(solution)/shard_map/all_to_all | solution.py:115
  296.8 18.4 %convolution_convert_fusion = bf16[512,5376]{1,0:T(8,128)(2,1)} fusion(bf16[512,2048]{0,1:T(8,128)(2,1)S(1)} %bitcast.37, bf16[2048,5376]{1,0:T(8,128)(2,1)} %param.7), kind=kOutput, calls=%fused_computation | convolution fusion | flops 11277041664 | bytes 29622272 | tf_op jit(solution)/shard_map/dot_general | solution.py:118
  315.2 0.0 reduce-scatter.2.cloned.1.call-update
  315.2 69.2 %reduce-scatter.2.cloned.1.call-done = bf16[256,5376]{1,0:T(8,128)(2,1)} async-done(((bf16[512,5376]{1,0:T(8,128)(2,1)}), bf16[256,5376]{1,0:T(8,128)(2,1)}) %reduce-scatter.2.cloned.1.call-update) | async-done | bytes 2752528 | tf_op jit(solution)/shard_map/reduce_scatter | solution.py:117
Async XLA Ops:
  9.9 7.6 %copy-start.1 = (bf16[512,1024]{1,0:T(8,128)(2,1)S(1)}, bf16[512,1024]{1,0:T(8,128)(2,1)}, u32[]{:S(2)}) copy-start(bf16[512,1024]{1,0:T(8,128)(2,1)} %param.6) | copy-start | bytes 3145732
  9.9 48.5 %all-to-all-start.1 = ((bf16[16,512,128]{2,1,0:T(8,128)(2,1)}), bf16[16,512,128]{2,1,0:T(8,128)(2,1)S(1)}, u32[]{:S(2)}, u32[]{:S(2)}) async-start(bf16[16,512,128]{2,1,0:T(8,128)(2,1)} %bitcast.4), calls=%async_computation.1 | async-start | bytes 4194304 | tf_op jit(solution)/shard_map/all_to_all | solution.py:111
  58.4 2.0 copy-start
  60.4 52.3 %all-to-all-start.2 = ((bf16[16,512,128]{2,1,0:T(8,128)(2,1)}), bf16[16,512,128]{2,1,0:T(8,128)(2,1)}, u32[]{:S(2)}, u32[]{:S(2)}) async-start(bf16[16,512,128]{2,1,0:T(8,128)(2,1)} %bitcast.7), calls=%async_computation.2 | async-start | bytes 4194304 | tf_op jit(solution)/shard_map/all_to_all | solution.py:111
  71.7 312.7 %reduce-scatter.2.cloned.1.call-start = ((), (), s32[]{:S(2)}) async-start(), calls=%async_computation.5 | async-start | bytes 8257536 | tf_op jit(solution)/shard_map/reduce_scatter | solution.py:117
Sparse Core Ops, SparseCore 0:
  315.3 69.0 reduce-scatter.1

commit v2 on v1

--- a/solution.py
+++ b/solution.py
@@ -94,32 +94,220 @@
     )(q, k, v)
 
 
+MESH = pl.DeviceIdType.MESH
+
+
+def greet(n):
+    me = lax.axis_index("seq")
+    barrier = pltpu.get_barrier_semaphore()
+
+    @pl.loop(1, n)
+    def _(d):
+        pl.semaphore_signal(
+            barrier, inc=1, device_id={"seq": lax.rem(me + d, n)}, device_id_type=MESH
+        )
+
+    pl.semaphore_wait(barrier, n - 1)
+    return me
+
+
+def remote(src, dst, send, recv, peer):
+    return pltpu.make_async_remote_copy(
+        src_ref=src,
+        dst_ref=dst,
+        send_sem=send,
+        recv_sem=recv,
+        device_id={"seq": peer},
+        device_id_type=MESH,
+    )
+
+
+def inbound(n, parts, width, dup, q_ref, k_ref, v_ref, q_o, k_o, v_o, send, recv, own, send2, recv2):
+    me = greet(n)
+    span = q_ref.shape[0]
+    frac = span // dup
+
+    def sources(j):
+        head = j // parts
+        rows = pl.ds(pl.multiple_of(lax.rem(j, parts) * width, width), width)
+        q = q_ref.at[rows, pl.ds(pl.multiple_of(head * HD, HD), HD)]
+        kv_rows = pl.ds(pl.multiple_of(lax.rem(j, dup) * frac, frac), frac)
+        kv_cols = pl.ds(pl.multiple_of(j // dup * HD, HD), HD)
+        return q, k_ref.at[kv_rows, kv_cols], v_ref.at[kv_rows, kv_cols]
+
+    def places(owner, j):
+        kv_rows = pl.ds(pl.multiple_of(lax.rem(j, dup) * frac, frac), frac)
+        return q_o.at[owner], k_o.at[owner, kv_rows], v_o.at[owner, kv_rows]
+
+    def copies(d):
+        peer = lax.rem(me + d, n)
+        pairs = zip(sources(peer), places(me, peer))
+        return [remote(x, y, send.at[i, d], recv.at[i, d], peer) for i, (x, y) in enumerate(pairs)]
+
+    @pl.loop(1, n)
+    def _(d):
+        for i in (1, 2, 0):
+            copies(d)[i].start()
+
+    local = [
+        pltpu.make_async_copy(x, y, own.at[i])
+        for i, (x, y) in enumerate(zip(sources(me), places(me, me)))
+    ]
+    for c in local:
+        c.start()
+    for c in local:
+        c.wait()
+
+    def arrived(i):
+        @pl.loop(1, n)
+        def _(d):
+            owner = lax.rem(me + n - d, n)
+            place = places(owner, me)[i]
+            remote(place, place, send.at[i, d], recv.at[i, d], owner).wait_recv()
+
+    arrived(1)
+    arrived(2)
+    base = me // dup * dup
+    mine = lax.rem(me, dup)
+
+    def shares(d):
+        peer = base + lax.rem(mine + d, dup)
+        rows = pl.ds(pl.multiple_of(mine * frac, frac), frac)
+        return [
+            remote(x.at[:, rows], x.at[:, rows], send2.at[i, d], recv2.at[i, d], peer)
+            for i, x in enumerate((k_o, v_o))
+        ]
+
+    for d in range(1, dup):
+        for c in shares(d):
+            c.start()
+    arrived(0)
+    for d in range(1, dup):
+        owner = lax.rem(mine + dup - d, dup)
+        rows = pl.ds(pl.multiple_of(owner * frac, frac), frac)
+        for i, x in enumerate((k_o, v_o)):
+            place = x.at[:, rows]
+            remote(place, place, send2.at[i, d], recv2.at[i, d], base + owner).wait_recv()
+        for c in shares(d):
+            c.wait_send()
+
+    @pl.loop(1, n)
+    def _(d):
+        for c in copies(d):
+            c.wait_send()
+
+
+def gather_heads(q, k, v, n, parts, width, dup):
+    span = q.shape[0]
+    any_space = pl.BlockSpec(memory_space=pl.ANY)
+    vmem = pl.BlockSpec(memory_space=pltpu.VMEM)
+    return pl.pallas_call(
+        functools.partial(inbound, n, parts, width, dup),
+        in_specs=[any_space] * 3,
+        out_specs=[vmem] * 3,
+        out_shape=[
+            jax.ShapeDtypeStruct((n, width, HD), jnp.bfloat16),
+            jax.ShapeDtypeStruct((n, span, HD), jnp.bfloat16),
+            jax.ShapeDtypeStruct((n, span, HD), jnp.bfloat16),
+        ],
+        scratch_shapes=[
+            pltpu.SemaphoreType.DMA((3, n)),
+            pltpu.SemaphoreType.DMA((3, n)),
+            pltpu.SemaphoreType.DMA((3,)),
+            pltpu.SemaphoreType.DMA((2, dup)),
+            pltpu.SemaphoreType.DMA((2, dup)),
+        ],
+        compiler_params=pltpu.CompilerParams(
+            collective_id=0, has_side_effects=True, vmem_limit_bytes=40 * 2**20
+        ),
+    )(q, k, v)
+
+
+def outbound(n, parts, width, x_ref, o_ref, send, recv, own):
+    me = greet(n)
+
+    def place(j):
+        rows = pl.ds(pl.multiple_of(lax.rem(j, parts) * width, width), width)
+        return o_ref.at[rows, pl.ds(pl.multiple_of(j // parts * HD, HD), HD)]
+
+    def copy(d):
+        peer = lax.rem(me + d, n)
+        return remote(x_ref.at[peer], place(me), send.at[d], recv.at[d], peer)
+
+    @pl.loop(1, n)
+    def _(d):
+        copy(d).start()
+
+    local = pltpu.make_async_copy(x_ref.at[me], place(me), own)
+    local.start()
+    local.wait()
+
+    @pl.loop(1, n)
+    def _(d):
+        owner = lax.rem(me + n - d, n)
+        there = place(owner)
+        remote(there, there, send.at[d], recv.at[d], owner).wait_recv()
+        copy(d).wait_send()
+
+
+def return_heads(x, n, parts, width, span, qh):
+    return pl.pallas_call(
+        functools.partial(outbound, n, parts, width),
+        in_specs=[pl.BlockSpec(memory_space=pl.ANY)],
+        out_specs=pl.BlockSpec(memory_space=pltpu.VMEM),
+        out_shape=jax.ShapeDtypeStruct((span, qh * HD), jnp.bfloat16),
+        scratch_shapes=[
+            pltpu.SemaphoreType.DMA((n,)),
+            pltpu.SemaphoreType.DMA((n,)),
+            pltpu.SemaphoreType.DMA,
+        ],
+        compiler_params=pltpu.CompilerParams(
+            collective_id=1, has_side_effects=True, vmem_limit_bytes=40 * 2**20
+        ),
+    )(x)
+
+
+def project(attended, out_weight):
+    heads = lax.axis_size("head")
+    mine = lax.axis_index("head")
+    rows = attended.shape[0] // heads
+    columns = out_weight.shape[1]
+    chunks = next(c for c in (6, 4, 3, 2, 1) if columns % (c * HD) == 0)
+    step = columns // chunks
+
+    def part(dest, c):
+        x = lax.dynamic_slice_in_dim(attended, dest * rows, rows, 0)
+        w = out_weight[:, c * step : (c + 1) * step]
+        return jnp.dot(x, w, preferred_element_type=jnp.float32)
+
+    done = []
+    received = []
+    for c in range(chunks):
+        got = []
+        for k in range(1, heads):
+            term = part(lax.rem(mine + k, heads), c).astype(jnp.bfloat16)
+            got.append(lax.ppermute(term, "head", [(i, (i + k) % heads) for i in range(heads)]))
+        received.append(got)
+    for c in range(chunks):
+        total = part(mine, c)
+        for got in received[c]:
+            total = total + got.astype(jnp.float32)
+        done.append(total.astype(jnp.bfloat16))
+    return jnp.concatenate(done, axis=1)
+
+
 def per_device(queries, key_rows, values, out_weight):
     n = lax.axis_size("seq")
-    heads = lax.axis_size("head")
-    mine = lax.axis_index("head")
     span = queries.shape[0]
     qh = queries.shape[1] // HD
     kvh = key_rows.shape[1] // HD
     parts = n // qh
     width = span // parts
-    q = queries.reshape(parts, width, qh, HD).transpose(2, 0, 1, 3).reshape(n, width, HD)
-
-    def spread(x):
-        x = x.reshape(span, kvh, HD).transpose(1, 0, 2)
-        x = jnp.repeat(x, n // kvh, axis=0)
-        return lax.all_to_all(x, "seq", 0, 0, tiled=True).reshape(n * span, HD)
-
-    q = lax.all_to_all(q, "seq", 0, 0, tiled=True).reshape(n * width, HD)
-    out = attention(q, spread(key_rows), spread(values), span, width, parts)
-    out = lax.all_to_all(out.reshape(n, width, HD), "seq", 0, 0, tiled=True)
-    attended = out.reshape(qh, parts, width, HD).transpose(1, 2, 0, 3).reshape(span, qh * HD)
-    return lax.psum_scatter(
-        jnp.dot(attended, out_weight, preferred_element_type=jnp.float32).astype(jnp.bfloat16),
-        "head",
-        scatter_dimension=0,
-        tiled=True,
-    )
+    q, k, v = gather_heads(queries, key_rows, values, n, parts, width, n // kvh)
+    q = q.reshape(n * width, HD)
+    out = attention(q, k.reshape(n * span, HD), v.reshape(n * span, HD), span, width, parts)
+    attended = return_heads(out.reshape(n, width, HD), n, parts, width, span, qh)
+    return project(attended, out_weight)
 
 
 def solution(mesh):

time: 392 us -> 297 us (0.76)
  the two profiles are of different devices: /device:TPU:0 before, /device:TPU:15 now
where the time goes in v2:
time: 297 us
  Pallas kernels  218 us (73%)
  matrix products  38.8 us (13%)
  waiting for transfers between devices  25.9 us (9%)
  local copies, waits for them, and re-layouts  9.61 us (3%)
  starting transfers between devices  4.53 us (2%)
    pallas_call x1, Pallas kernels, gather_heads(): pl.pallas_call(functools.partial(inbound, n, parts, width, dup), in_specs...  97 us
    pallas_call x1, Pallas kernels, attention(): pl.pallas_call(functools.partial(attn_kernel, span, width, parts, bq, bkv...  70.8 us
    pallas_call x1, Pallas kernels, return_heads(): pl.pallas_call(functools.partial(outbound, n, parts, width), in_specs=[pl...  50.2 us
    dot_general x12, matrix products, part(): return jnp.dot(x, w, preferred_element_type=jnp.float32)  38.8 us
    ppermute x6, waiting for transfers between devices, project(): lax.ppermute(term, 'head', [(i, (i + k) % heads) for i in range(heads)])  25.9 us
    unnamed x18, local copies, waits for them, and re-layouts  9.61 us
  transfers between devices with their start and end apart: 6, of which 5 were waited for; matrix products, arithmetic and copies ran while one was open for 10% of the time, Pallas kernels for 0%

profile of v2, /device:TPU:15, one launch (start us, length us, event | category | flops | bytes accessed | tf_op | source)
XLA Modules:
  0.0 297.1 jit_solution(17414620458703050392)
XLA Ops:
  0.0 0.0 copy-start.1
  0.0 1.6 copy-done.1
  1.6 0.0 copy-start.5
  1.6 1.2 copy-done.5
  2.8 0.0 copy-start.6
  2.8 1.2 copy-done.6
  4.0 97.0 %shard_map.46 = (bf16[16,512,128]{2,1,0:T(8,128)(2,1)S(1)}, bf16[16,512,128]{2,1,0:T(8,128)(2,1)S(1)}, bf16[16,512,128]{2,1,0:T(8,128)(2,1)S(1)}) custom-call(bf16[512,2048]{1,0:T(8,128)(2,1)S(1)} %copy-done.1, bf16[512,1024]{1,0:T(8,128)(2,1)S(1)} %copy-done.5, bf16[512,1024]{1,0:T(8,128)(2,1)S(1)} %copy-done.6), custom_call_target="tpu_custom_call" | custom-call | tf_op jit(solution)/shard_map/pallas_call | solution.py:204
  101.1 0.0 copy-start.2
  101.1 1.3 copy-done.2
  102.4 0.0 copy-start.3
  102.4 1.3 copy-done.3
  103.7 0.0 copy-start.4
  103.8 1.3 copy-done.4
  105.1 70.8 %shard_map.47 = bf16[8192,128]{1,0:T(8,128)(2,1)} custom-call(bf16[8192,128]{1,0:T(8,128)(2,1)} %bitcast.5, bf16[8192,128]{1,0:T(8,128)(2,1)} %bitcast.6, bf16[8192,128]{1,0:T(8,128)(2,1)} %bitcast.7), custom_call_target="tpu_custom_call" | custom-call | tf_op jit(solution)/shard_map/pallas_call | solution.py:77
  175.9 0.0 copy-start
  175.9 1.6 copy-done
  177.5 50.2 %shard_map.48 = bf16[512,2048]{1,0:T(8,128)(2,1)S(1)} custom-call(bf16[16,512,128]{2,1,0:T(8,128)(2,1)S(1)} %bitcast.4), custom_call_target="tpu_custom_call" | custom-call | tf_op jit(solution)/shard_map/pallas_call | solution.py:254
  227.7 0.0 copy-start.7
  227.7 4.2 %fusion.24 = bf16[256,896]{1,0:T(8,128)(2,1)} fusion(bf16[2048,5376]{1,0:T(8,128)(2,1)} %param.7, bf16[512,2048]{1,0:T(8,128)(2,1)S(1)} %shard_map.48, s32[]{:T(128)S(6)} %select_n.5), kind=kOutput, calls=%fused_computation.24 | convolution fusion | flops 939753472 | bytes 5177348 | tf_op jit(solution)/shard_map/dot_general | solution.py:281
  232.0 0.2 collective-permute-start
  232.2 4.8 %fusion.27 = bf16[256,896]{1,0:T(8,128)(2,1)} fusion(bf16[2048,5376]{1,0:T(8,128)(2,1)} %param.7, bf16[512,2048]{1,0:T(8,128)(2,1)S(1)} %shard_map.48, s32[]{:T(128)S(6)} %select_n.5), kind=kOutput, calls=%fused_computation.25 | convolution fusion | flops 939753472 | bytes 5177348 | tf_op jit(solution)/shard_map/dot_general | solution.py:281
  237.0 1.2 collective-permute-start.1
  238.2 4.1 %fusion.30 = bf16[256,896]{1,0:T(8,128)(2,1)} fusion(bf16[2048,5376]{1,0:T(8,128)(2,1)} %param.7, bf16[512,2048]{1,0:T(8,128)(2,1)S(1)} %shard_map.48, s32[]{:T(128)S(6)} %select_n.5), kind=kOutput, calls=%fused_computation.26 | convolution fusion | flops 939753472 | bytes 5177348 | tf_op jit(solution)/shard_map/dot_general | solution.py:281
  242.3 0.3 collective-permute-start.2
  242.6 0.0 copy-done.7
  242.6 2.1 fusion.33
  244.6 1.2 collective-permute-start.3
  245.8 1.3 fusion.36
  247.2 0.3 collective-permute-start.4
  247.5 1.3 fusion.39
  248.8 0.0 collective-permute-done
  248.8 1.3 collective-permute-start.5
  250.1 3.4 %fusion.42 = bf16[256,5376]{1,0:T(8,128)(2,1)S(1)} fusion(bf16[256,896]{1,0:T(8,128)(2,1)} %collective-permute-done, bf16[2048,5376]{1,0:T(8,128)(2,1)} %param.7, bf16[512,2048]{1,0:T(8,128)(2,1)S(1)} %shard_map.48, s32[]{:T(128)S(6)} %select_n.4), kind=kOutput, calls=%fused_computation.36 | convolution fusion | flops 940212224 | bytes 5636100 | tf_op jit(solution)/shard_map/dot_general | solution.py:281
  253.5 1.2 collective-permute-done.1
  254.6 3.4 %fusion.43 = bf16[256,5376]{1,0:T(8,128)(2,1)S(1)} fusion(bf16[256,5376]{1,0:T(8,128)(2,1)S(1)} %fusion.42, bf16[256,896]{1,0:T(8,128)(2,1)} %collective-permute-done.1, bf16[2048,5376]{1,0:T(8,128)(2,1)} %param.7, bf16[512,2048]{1,0:T(8,128)(2,1)S(1)} %shard_map.48, s32[]{:T(128)S(6)} %select_n.4), kind=kOutput, calls=%fused_computation.37 | convolution fusion | flops 940212224 | bytes 5636100 | tf_op jit(solution)/shard_map/dot_general | solution.py:281
  258.1 6.4 %collective-permute-done.2 = bf16[256,896]{1,0:T(8,128)(2,1)} collective-permute-done((bf16[256,896]{1,0:T(8,128)(2,1)}, bf16[256,896]{1,0:T(8,128)(2,1)}, u32[]{:S(2)}, u32[]{:S(2)}) %collective-permute-start.2) | collective-permute-done | bytes 458784 | tf_op jit(solution)/shard_map/ppermute | solution.py:289
  264.5 3.4 %fusion.44 = bf16[256,5376]{1,0:T(8,128)(2,1)S(1)} fusion(bf16[256,5376]{1,0:T(8,128)(2,1)S(1)} %fusion.43, bf16[256,896]{1,0:T(8,128)(2,1)} %collective-permute-done.2, bf16[2048,5376]{1,0:T(8,128)(2,1)} %param.7, bf16[512,2048]{1,0:T(8,128)(2,1)S(1)} %shard_map.48, s32[]{:T(128)S(6)} %select_n.4), kind=kOutput, calls=%fused_computation.38 | convolution fusion | flops 940212224 | bytes 5636100 | tf_op jit(solution)/shard_map/dot_general | solution.py:281
  267.9 6.3 %collective-permute-done.3 = bf16[256,896]{1,0:T(8,128)(2,1)} collective-permute-done((bf16[256,896]{1,0:T(8,128)(2,1)}, bf16[256,896]{1,0:T(8,128)(2,1)}, u32[]{:S(2)}, u32[]{:S(2)}) %collective-permute-start.3) | collective-permute-done | bytes 458784 | tf_op jit(solution)/shard_map/ppermute | solution.py:289
  274.2 3.4 %fusion.45 = bf16[256,5376]{1,0:T(8,128)(2,1)S(1)} fusion(bf16[256,5376]{1,0:T(8,128)(2,1)S(1)} %fusion.44, bf16[256,896]{1,0:T(8,128)(2,1)} %collective-permute-done.3, bf16[2048,5376]{1,0:T(8,128)(2,1)} %param.7, bf16[512,2048]{1,0:T(8,128)(2,1)S(1)} %shard_map.48, s32[]{:T(128)S(6)} %select_n.4), kind=kOutput, calls=%fused_computation.39 | convolution fusion | flops 940212224 | bytes 5636100 | tf_op jit(solution)/shard_map/dot_general | solution.py:281
  277.6 6.4 %collective-permute-done.4 = bf16[256,896]{1,0:T(8,128)(2,1)S(1)} collective-permute-done((bf16[256,896]{1,0:T(8,128)(2,1)S(1)}, bf16[256,896]{1,0:T(8,128)(2,1)S(1)}, u32[]{:S(2)}, u32[]{:S(2)}) %collective-permute-start.4) | collective-permute-done | bytes 458784 | tf_op jit(solution)/shard_map/ppermute | solution.py:289
  284.0 3.3 %fusion.46 = bf16[256,5376]{1,0:T(8,128)(2,1)S(1)} fusion(bf16[256,5376]{1,0:T(8,128)(2,1)S(1)} %fusion.45, bf16[256,896]{1,0:T(8,128)(2,1)S(1)} %collective-permute-done.4, bf16[2048,5376]{1,0:T(8,128)(2,1)} %param.7, bf16[512,2048]{1,0:T(8,128)(2,1)S(1)} %shard_map.48, s32[]{:T(128)S(6)} %select_n.4), kind=kOutput, calls=%fused_computation.40 | convolution fusion | flops 940212224 | bytes 5636100 | tf_op jit(solution)/shard_map/dot_general | solution.py:281
  287.4 0.0 copy-start.8
  287.4 5.6 %collective-permute-done.5 = bf16[256,896]{1,0:T(8,128)(2,1)S(1)} collective-permute-done((bf16[256,896]{1,0:T(8,128)(2,1)S(1)}, bf16[256,896]{1,0:T(8,128)(2,1)S(1)}, u32[]{:S(2)}, u32[]{:S(2)}) %collective-permute-start.5) | collective-permute-done | bytes 458784 | tf_op jit(solution)/shard_map/ppermute | solution.py:289
  293.0 0.0 copy-done.8
  293.0 4.1 %fusion.47 = bf16[256,5376]{1,0:T(8,128)(2,1)} fusion(bf16[256,5376]{1,0:T(8,128)(2,1)} %copy-done.8, bf16[256,896]{1,0:T(8,128)(2,1)S(1)} %collective-permute-done.5, bf16[2048,5376]{1,0:T(8,128)(2,1)} %param.7, bf16[512,2048]{1,0:T(8,128)(2,1)S(1)} %shard_map.48, s32[]{:T(128)S(6)} %select_n.4), kind=kOutput, calls=%fused_computation.41 | convolution fusion | flops 940212224 | bytes 5636100 | tf_op jit(solution)/shard_map/dot_general | solution.py:281
Async XLA Ops:
  0.0 1.6 copy-start.1
  1.6 1.2 copy-start.5
  2.8 1.2 copy-start.6
  101.1 1.3 copy-start.2
  102.4 1.3 copy-start.3
  103.7 1.3 copy-start.4
  175.9 1.6 copy-start
  227.7 14.8 %copy-start.7 = (bf16[2048,5376]{1,0:T(8,128)(2,1)S(1)}, bf16[2048,5376]{1,0:T(8,128)(2,1)}, u32[]{:S(2)}) copy-start(bf16[2048,5376]{1,0:T(8,128)(2,1)} %param.7) | copy-start | bytes 66060292
  232.0 16.8 %collective-permute-start = (bf16[256,896]{1,0:T(8,128)(2,1)}, bf16[256,896]{1,0:T(8,128)(2,1)}, u32[]{:S(2)}, u32[]{:S(2)}) collective-permute-start(bf16[256,896]{1,0:T(8,128)(2,1)} %fusion.24), channel_id=1, source_target_pairs={{0,1},{1,0},{2,3},{3,2},{4,5},{5,4},{6,7},{7,6},{8,9},{9,8},{10,11... | collective-permute-start | bytes 1376264 | tf_op jit(solution)/shard_map/ppermute | solution.py:289
  237.0 17.6 %collective-permute-start.1 = (bf16[256,896]{1,0:T(8,128)(2,1)}, bf16[256,896]{1,0:T(8,128)(2,1)}, u32[]{:S(2)}, u32[]{:S(2)}) collective-permute-start(bf16[256,896]{1,0:T(8,128)(2,1)} %fusion.27), channel_id=1, source_target_pairs={{0,1},{1,0},{2,3},{3,2},{4,5},{5,4},{6,7},{7,6},{8,9},{9,8},{10,11... | collective-permute-start | bytes 1376264 | tf_op jit(solution)/shard_map/ppermute | solution.py:289
  242.3 22.2 %collective-permute-start.2 = (bf16[256,896]{1,0:T(8,128)(2,1)}, bf16[256,896]{1,0:T(8,128)(2,1)}, u32[]{:S(2)}, u32[]{:S(2)}) collective-permute-start(bf16[256,896]{1,0:T(8,128)(2,1)} %fusion.30), channel_id=1, source_target_pairs={{0,1},{1,0},{2,3},{3,2},{4,5},{5,4},{6,7},{7,6},{8,9},{9,8},{10,11... | collective-permute-start | bytes 1376264 | tf_op jit(solution)/shard_map/ppermute | solution.py:289
  244.6 29.6 %collective-permute-start.3 = (bf16[256,896]{1,0:T(8,128)(2,1)}, bf16[256,896]{1,0:T(8,128)(2,1)}, u32[]{:S(2)}, u32[]{:S(2)}) collective-permute-start(bf16[256,896]{1,0:T(8,128)(2,1)} %fusion.33), channel_id=1, source_target_pairs={{0,1},{1,0},{2,3},{3,2},{4,5},{5,4},{6,7},{7,6},{8,9},{9,8},{10,11... | collective-permute-start | bytes 1376264 | tf_op jit(solution)/shard_map/ppermute | solution.py:289
  247.2 36.9 %collective-permute-start.4 = (bf16[256,896]{1,0:T(8,128)(2,1)S(1)}, bf16[256,896]{1,0:T(8,128)(2,1)S(1)}, u32[]{:S(2)}, u32[]{:S(2)}) collective-permute-start(bf16[256,896]{1,0:T(8,128)(2,1)S(1)} %fusion.36), channel_id=1, source_target_pairs={{0,1},{1,0},{2,3},{3,2},{4,5},{5,4},{6,7},{7,6},{8,9},{9,8},{10,11... | collective-permute-start | bytes 1376264 | tf_op jit(solution)/shard_map/ppermute | solution.py:289
  248.8 44.2 %collective-permute-start.5 = (bf16[256,896]{1,0:T(8,128)(2,1)S(1)}, bf16[256,896]{1,0:T(8,128)(2,1)S(1)}, u32[]{:S(2)}, u32[]{:S(2)}) collective-permute-start(bf16[256,896]{1,0:T(8,128)(2,1)S(1)} %fusion.39), channel_id=1, source_target_pairs={{0,1},{1,0},{2,3},{3,2},{4,5},{5,4},{6,7},{7,6},{8,9},{9,8},{10,11... | collective-permute-start | bytes 1376264 | tf_op jit(solution)/shard_map/ppermute | solution.py:289
  287.4 5.6 %copy-start.8 = (bf16[256,5376]{1,0:T(8,128)(2,1)}, bf16[256,5376]{1,0:T(8,128)(2,1)S(1)}, u32[]{:S(2)}) copy-start(bf16[256,5376]{1,0:T(8,128)(2,1)S(1)} %fusion.46) | copy-start | bytes 8257540

commit v3 on v2

v3 whole, which is shorter than its diff:
```python
import functools
import math

import jax
import jax.numpy as jnp
from jax import lax
from jax.experimental import pallas as pl
from jax.experimental.pallas import tpu as pltpu
from jax.sharding import PartitionSpec as P

HD = 128
SCALE = 168.0 ** (-0.5) * math.log2(math.e)
NEG = -1e30


def attn_body(lay, phase, q_ref, k_ref, v_ref, o_ref, kt, v1, m_s, acc_s):
    n, parts, runs, run_rows, ph, span = lay
    total = k_ref.shape[0]
    rows_each = runs * ph
    count = q_ref.shape[0]
    bq = math.gcd(count, 1024)
    bkv = math.gcd(total, 1024)
    pieces = 4
    step = bq // pieces
    sub = lax.rem(lax.axis_index("seq"), parts)
    reach = bq // rows_each * span

    @pl.loop(0, total // bkv)
    def _(b):
        rows = pl.ds(pl.multiple_of(b * bkv, bkv), bkv)
        flipped = k_ref[rows, :].T
        kt[:HD, rows] = flipped
        kt[HD:, rows] = flipped
        v1[rows, :HD] = v_ref[rows, :]
        v1[rows, HD:] = jnp.ones((bkv, HD), jnp.bfloat16)

    @pl.loop(0, count // bq)
    def _(i):
        here = pl.ds(pl.multiple_of(i * bq, bq), bq)
        qf = q_ref[here, :].astype(jnp.float32) * SCALE
        high = qf.astype(jnp.bfloat16)
        low = (qf - high.astype(jnp.float32)).astype(jnp.bfloat16)
        q2 = jnp.concatenate([high, low], axis=1)
        m_s[...] = jnp.full_like(m_s, NEG)
        acc_s[...] = jnp.zeros_like(acc_s)

        def piece(t, start, masked):
            cols = pl.ds(pl.multiple_of(start, bkv), bkv)
            rows = slice(t * step, (t + 1) * step)
            s = jnp.dot(q2[rows], kt[:, cols], preferred_element_type=jnp.float32)
            if masked:
                row = i * bq + t * step + lax.broadcasted_iota(jnp.int32, (step, 1), 0)
                run = sub * runs + row // ph % runs
                pos = row // rows_each * span + run * run_rows + phase * ph + row % ph
                col = start + lax.broadcasted_iota(jnp.int32, (1, bkv), 1)
                s = jnp.where(col <= pos, s, NEG)
            m0 = m_s[rows, :]
            m1 = jnp.maximum(m0, jnp.max(s, axis=1, keepdims=True))
            m_s[rows, :] = m1
            p = jnp.exp2(s - jnp.tile(m1, (1, bkv // HD))).astype(jnp.bfloat16)
            f = jnp.exp2(m0 - m1)
            acc_s[rows, :] = acc_s[rows, :] * jnp.tile(f, (1, 2)) + jnp.dot(
                p, v1[cols, :], preferred_element_type=jnp.float32
            )

        def whole(j, c):
            for t in range(pieces):
                piece(t, j * bkv, False)
            return c

        lax.fori_loop(0, i * (reach // bkv), whole, 0)
        for j in range(reach // bkv):
            for t in range(pieces):
                first = t * step // rows_each * span
                last = (((t + 1) * step - 1) // rows_each + 1) * span
                if j * bkv < last:
                    piece(t, i * reach + j * bkv, first < (j + 1) * bkv)
        out = acc_s[...]
        o_ref[here, :] = (out[:, :HD] / out[:, HD:]).astype(o_ref.dtype)


def query_source(lay, x, phase, j):
    n, parts, runs, run_rows, ph, span = lay
    return x.at[
        pl.ds(lax.rem(j, parts) * runs, runs),
        pl.ds(phase * ph, ph),
        pl.ds(pl.multiple_of(j // parts * HD, HD), HD),
    ]


def head_place(lay, x, j):
    n, parts, runs, run_rows, ph, span = lay
    return x.at[
        pl.ds(lax.rem(j, parts) * runs, runs),
        slice(None),
        pl.ds(pl.multiple_of(j // parts * HD, HD), HD),
    ]


def attn_kernel(lay, phase, carry, q_ref, k_ref, v_ref, x_ref, o_ref, y_ref, kt, v1, m_s, acc_s, *sems):
    n = lay[0]
    me = greet(n)
    if carry == "queries":
        exchange = (lambda j: query_source(lay, x_ref, phase + 1, j)), (lambda j: y_ref.at[j])
    else:
        exchange = (lambda j: x_ref.at[j]), (lambda j: head_place(lay, y_ref, j))
    begin_exchange(n, me, *exchange, *sems)
    attn_body(lay, phase, q_ref, k_ref, v_ref, o_ref, kt, v1, m_s, acc_s)
    end_exchange(n, me, *exchange, *sems)


def attention(lay, phase, carry, q, k, v, x, y_shape):
    n, parts, runs, run_rows, ph, span = lay
    rows, total = q.shape[0], k.shape[0]
    bq = math.gcd(rows, 1024)
    vmem = pl.BlockSpec(memory_space=pltpu.VMEM)
    return pl.pallas_call(
        functools.partial(attn_kernel, lay, phase, carry),
        in_specs=[vmem, vmem, vmem, pl.BlockSpec(memory_space=pl.ANY)],
        out_specs=[vmem, vmem],
        out_shape=[
            jax.ShapeDtypeStruct((rows, HD), jnp.bfloat16),
            jax.ShapeDtypeStruct(y_shape, jnp.bfloat16),
        ],
        scratch_shapes=[
            pltpu.VMEM((2 * HD, total), jnp.bfloat16),
            pltpu.VMEM((total, 2 * HD), jnp.bfloat16),
            pltpu.VMEM((bq, HD), jnp.float32),
            pltpu.VMEM((bq, 2 * HD), jnp.float32),
            pltpu.SemaphoreType.DMA((n,)),
            pltpu.SemaphoreType.DMA((n,)),
            pltpu.SemaphoreType.DMA,
        ],
        compiler_params=pltpu.CompilerParams(
            collective_id=2 + phase, has_side_effects=True, vmem_limit_bytes=50 * 2**20
        ),
    )(q, k, v, x)


MESH = pl.DeviceIdType.MESH


def greet(n, others=0):
    me = lax.axis_index("seq")
    barrier = pltpu.get_barrier_semaphore()

    @pl.loop(1, n)
    def _(d):
        pl.semaphore_signal(
            barrier, inc=1, device_id={"seq": lax.rem(me + d, n)}, device_id_type=MESH
        )

    pl.semaphore_wait(barrier, n - 1 + others)
    return me


def remote(src, dst, send, recv, peer):
    return pltpu.make_async_remote_copy(
        src_ref=src,
        dst_ref=dst,
        send_sem=send,
        recv_sem=recv,
        device_id={"seq": peer},
        device_id_type=MESH,
    )


def inbound(lay, dup, q_ref, k_ref, v_ref, q_o, k_o, v_o, send, recv, own, send2, recv2):
    n, parts, runs, run_rows, ph, span = lay
    me = greet(n)
    frac = span // dup

    def sources(j):
        q = query_source(lay, q_ref, 0, j)
        kv_rows = pl.ds(pl.multiple_of(lax.rem(j, dup) * frac, frac), frac)
        kv_cols = pl.ds(pl.multiple_of(j // dup * HD, HD), HD)
        return q, k_ref.at[kv_rows, kv_cols], v_ref.at[kv_rows, kv_cols]

    def places(owner, j):
        kv_rows = pl.ds(pl.multiple_of(lax.rem(j, dup) * frac, frac), frac)
        return q_o.at[owner], k_o.at[owner, kv_rows], v_o.at[owner, kv_rows]

    def copies(d):
        peer = lax.rem(me + d, n)
        pairs = zip(sources(peer), places(me, peer))
        return [remote(x, y, send.at[i, d], recv.at[i, d], peer) for i, (x, y) in enumerate(pairs)]

    @pl.loop(1, n)
    def _(d):
        for i in (1, 2, 0):
            copies(d)[i].start()

    local = [
        pltpu.make_async_copy(x, y, own.at[i])
        for i, (x, y) in enumerate(zip(sources(me), places(me, me)))
    ]
    for c in local:
        c.start()
    for c in local:
        c.wait()

    def arrived(i):
        @pl.loop(1, n)
        def _(d):
            owner = lax.rem(me + n - d, n)
            place = places(owner, me)[i]
            remote(place, place, send.at[i, d], recv.at[i, d], owner).wait_recv()

    arrived(1)
    arrived(2)
    base = me // dup * dup
    mine = lax.rem(me, dup)

    def shares(d):
        peer = base + lax.rem(mine + d, dup)
        rows = pl.ds(pl.multiple_of(mine * frac, frac), frac)
        return [
            remote(x.at[:, rows], x.at[:, rows], send2.at[i, d], recv2.at[i, d], peer)
            for i, x in enumerate((k_o, v_o))
        ]

    for d in range(1, dup):
        for c in shares(d):
            c.start()
    arrived(0)
    for d in range(1, dup):
        owner = lax.rem(mine + dup - d, dup)
        rows = pl.ds(pl.multiple_of(owner * frac, frac), frac)
        for i, x in enumerate((k_o, v_o)):
            place = x.at[:, rows]
            remote(place, place, send2.at[i, d], recv2.at[i, d], base + owner).wait_recv()
        for c in shares(d):
            c.wait_send()

    @pl.loop(1, n)
    def _(d):
        for c in copies(d):
            c.wait_send()


def gather_heads(lay, q, k, v, dup):
    n, parts, runs, run_rows, ph, span = lay
    any_space = pl.BlockSpec(memory_space=pl.ANY)
    vmem = pl.BlockSpec(memory_space=pltpu.VMEM)
    return pl.pallas_call(
        functools.partial(inbound, lay, dup),
        in_specs=[any_space] * 3,
        out_specs=[vmem] * 3,
        out_shape=[
            jax.ShapeDtypeStruct((n, runs, ph, HD), jnp.bfloat16),
            jax.ShapeDtypeStruct((n, span, HD), jnp.bfloat16),
            jax.ShapeDtypeStruct((n, span, HD), jnp.bfloat16),
        ],
        scratch_shapes=[
            pltpu.SemaphoreType.DMA((3, n)),
            pltpu.SemaphoreType.DMA((3, n)),
            pltpu.SemaphoreType.DMA((3,)),
            pltpu.SemaphoreType.DMA((2, dup)),
            pltpu.SemaphoreType.DMA((2, dup)),
        ],
        compiler_params=pltpu.CompilerParams(
            collective_id=0, has_side_effects=True, vmem_limit_bytes=40 * 2**20
        ),
    )(q, k, v)


def begin_exchange(n, me, source, place, send, recv, own):
    @pl.loop(1, n)
    def _(d):
        peer = lax.rem(me + d, n)
        remote(source(peer), place(me), send.at[d], recv.at[d], peer).start()

    pltpu.make_async_copy(source(me), place(me), own).start()


def end_exchange(n, me, source, place, send, recv, own):
    pltpu.make_async_copy(source(me), place(me), own).wait()

    @pl.loop(1, n)
    def _(d):
        owner = lax.rem(me + n - d, n)
        peer = lax.rem(me + d, n)
        there = place(owner)
        remote(there, there, send.at[d], recv.at[d], owner).wait_recv()
        remote(source(peer), place(me), send.at[d], recv.at[d], peer).wait_send()


def outbound(lay, heads, x_ref, t_ref, o_ref, g_ref, send, recv, own, send_x, recv_x):
    n = lay[0]
    mine = lax.axis_index("head")
    barrier = pltpu.get_barrier_semaphore()
    for k in range(1, heads):
        pl.semaphore_signal(
            barrier, inc=1, device_id={"head": lax.rem(mine + k, heads)}, device_id_type=MESH
        )
    me = greet(n, heads - 1)

    def term(k):
        return pltpu.make_async_remote_copy(
            src_ref=t_ref.at[k - 1],
            dst_ref=g_ref.at[k - 1],
            send_sem=send_x.at[k],
            recv_sem=recv_x.at[k],
            device_id={"head": lax.rem(mine + k, heads)},
            device_id_type=MESH,
        )

    exchange = (lambda j: x_ref.at[j]), (lambda j: head_place(lay, o_ref, j))
    for k in range(1, heads):
        term(k).start()
    begin_exchange(n, me, *exchange, send, recv, own)
    end_exchange(n, me, *exchange, send, recv, own)
    for k in range(1, heads):
        term(k).wait()


def return_heads(lay, x, shape, terms):
    n = lay[0]
    heads = lax.axis_size("head")
    space = pl.BlockSpec(memory_space=pl.ANY)
    return pl.pallas_call(
        functools.partial(outbound, lay, heads),
        in_specs=[space, space],
        out_specs=[pl.BlockSpec(memory_space=pltpu.VMEM), space],
        out_shape=[
            jax.ShapeDtypeStruct(shape, jnp.bfloat16),
            jax.ShapeDtypeStruct(terms.shape, jnp.bfloat16),
        ],
        scratch_shapes=[
            pltpu.SemaphoreType.DMA((n,)),
            pltpu.SemaphoreType.DMA((n,)),
            pltpu.SemaphoreType.DMA,
            pltpu.SemaphoreType.DMA((heads,)),
            pltpu.SemaphoreType.DMA((heads,)),
        ],
        compiler_params=pltpu.CompilerParams(
            collective_id=1, has_side_effects=True, vmem_limit_bytes=40 * 2**20
        ),
    )(x, terms)


def dot_rows(attended, out_weight, dest, columns):
    rows = attended.shape[0] // lax.axis_size("head")
    x = lax.dynamic_slice_in_dim(attended, dest * rows, rows, 0)
    return jnp.dot(x, out_weight[:, columns], preferred_element_type=jnp.float32)


def peer_terms(attended, out_weight, columns):
    heads = lax.axis_size("head")
    mine = lax.axis_index("head")
    return [
        dot_rows(attended, out_weight, lax.rem(mine + k, heads), columns).astype(jnp.bfloat16)
        for k in range(1, heads)
    ]


def project_end(attended, out_weight, columns, got):
    total = dot_rows(attended, out_weight, lax.axis_index("head"), columns)
    for term in got:
        total = total + term.astype(jnp.float32)
    return total.astype(jnp.bfloat16)


def project_last(attended, out_weight, chunks):
    heads = lax.axis_size("head")
    step = out_weight.shape[1] // chunks
    cuts = [slice(c * step, (c + 1) * step) for c in range(chunks)]
    received = [
        [
            lax.ppermute(term, "head", [(i, (i + k) % heads) for i in range(heads)])
            for k, term in enumerate(peer_terms(attended, out_weight, cut), 1)
        ]
        for cut in cuts
    ]
    done = [project_end(attended, out_weight, cut, got) for cut, got in zip(cuts, received)]
    return jnp.concatenate(done, axis=1)


def per_device(queries, key_rows, values, out_weight):
    n = lax.axis_size("seq")
    heads = lax.axis_size("head")
    span = queries.shape[0]
    qh = queries.shape[1] // HD
    kvh = key_rows.shape[1] // HD
    parts = n // qh
    runs = max(1, heads // parts)
    groups = parts * runs
    run_rows = span // groups
    phases = 2
    ph = run_rows // phases
    lay = (n, parts, runs, run_rows, ph, span)
    columns = out_weight.shape[1]
    chunks = 3 if columns % (3 * HD) == 0 else 1
    grid = queries.reshape(groups, run_rows, qh * HD)
    q0, k, v = gather_heads(lay, grid, key_rows, values, n // kvh)
    k = k.reshape(n * span, HD)
    v = v.reshape(n * span, HD)
    own = (n, runs, ph, HD)
    back = (groups, ph, qh * HD)
    out0, q1 = attention(lay, 0, "queries", q0.reshape(-1, HD), k, v, grid, own)
    out1, att0 = attention(lay, 1, "heads", q1.reshape(-1, HD), k, v, out0.reshape(own), back)
    att0 = att0.reshape(groups * ph, qh * HD)
    every = slice(0, columns)
    terms = jnp.stack(peer_terms(att0, out_weight, every))
    att1, got = return_heads(lay, out1.reshape(own), back, terms)
    second = project_last(att1.reshape(groups * ph, qh * HD), out_weight, chunks)
    first = project_end(att0, out_weight, every, [got[k] for k in range(heads - 1)])
    ends = [x.reshape(groups // heads, 1, ph, columns) for x in (first, second)]
    return jnp.concatenate(ends, axis=1).reshape(span // heads, columns)


def solution(mesh):
    placed = (P("seq", "head"), P("seq", "head"), P("seq", "head"), P("head", None))
    return jax.shard_map(
        per_device, mesh=mesh, in_specs=placed, out_specs=P(("seq", "head"), None), check_vma=False
    )
```

time: 297 us -> 256 us (0.86)
  the two profiles are of different devices: /device:TPU:15 before, /device:TPU:0 now
where the time goes in v3:
time: 256 us; the launch traced here: 255 us
  Pallas kernels  194 us (76%)
  matrix products  48.8 us (19%)
  local copies, waits for them, and re-layouts  7.66 us (3%)
  starting transfers between devices  2.56 us (1%)
    pallas_call x2, Pallas kernels, attention(): pl.pallas_call(functools.partial(attn_kernel, lay, phase, carry), in_spec...  99.2 us
    pallas_call x1, Pallas kernels, gather_heads(): pl.pallas_call(functools.partial(inbound, lay, dup), in_specs=[any_space]...  58.1 us
    dot_general x8, matrix products, dot_rows(): jnp.dot(x, out_weight[:, columns], preferred_element_type=jnp.float32)  48.8 us
    pallas_call x1, Pallas kernels, return_heads(): pl.pallas_call(functools.partial(outbound, lay, heads), in_specs=[space,...  36.5 us
    unnamed x16, local copies, waits for them, and re-layouts  7.66 us
  transfers between devices with their start and end apart: 3, of which 1 were waited for; matrix products, arithmetic and copies ran while one was open for 11% of the time, Pallas kernels for 0%

profile of v3, /device:TPU:0, one launch (start us, length us, event | category | flops | bytes accessed | tf_op | source)
XLA Modules:
  0.0 255.2 jit_solution(10542006749018127800)
XLA Ops:
  0.0 0.0 copy-start.2
  0.0 1.6 copy-done.2
  1.6 0.0 copy-start.3
  1.6 1.2 copy-done.3
  2.8 0.0 copy-start.4
  2.8 1.2 copy-done.4
  4.0 58.1 %shard_map.46 = (bf16[16,2,128,128]{3,2,1,0:T(8,128)(2,1)S(1)}, bf16[16,512,128]{2,1,0:T(8,128)(2,1)S(1)}, bf16[16,512,128]{2,1,0:T(8,128)(2,1)S(1)}) custom-call(bf16[2,256,2048]{2,1,0:T(8,128)(2,1)S(1)} %bitcast.26, bf16[512,1024]{1,0:T(8,128)(2,1)S(1)} %copy-done.3, bf16[512,1024]{1,0:T(8,128)(2,1)S(1)} %copy-done.4), custom_call_target="tpu_custom_call" | custom-call | tf_op jit(solution)/shard_map/pallas_call | solution.py:245
  62.2 0.0 copy-start
  62.2 1.3 copy-done
  63.5 0.0 copy-start.1
  63.5 1.3 copy-done.1
  64.8 61.2 %shard_map.47 = (bf16[4096,128]{1,0:T(8,128)(2,1)S(1)}, bf16[16,2,128,128]{3,2,1,0:T(8,128)(2,1)S(1)}) custom-call(bf16[4096,128]{1,0:T(8,128)(2,1)S(1)} %bitcast.29, bf16[8192,128]{1,0:T(8,128)(2,1)} %bitcast.21, bf16[8192,128]{1,0:T(8,128)(2,1)} %bitcast.23, bf16[2,256,2048]{2,1,0:T(8,128)(2,1)} %bitcast.25), custom_call_target="tpu_custom_call" | custom-call | tf_op jit(solution)/shard_map/pallas_call | solution.py:117
  126.0 0.0 copy-start.5
  126.0 1.0 copy-done.5
  127.0 38.1 %shard_map.48 = (bf16[4096,128]{1,0:T(8,128)(2,1)S(1)}, bf16[2,128,2048]{2,1,0:T(8,128)(2,1)S(1)}) custom-call(bf16[4096,128]{1,0:T(8,128)(2,1)S(1)} %bitcast.32, bf16[8192,128]{1,0:T(8,128)(2,1)} %bitcast.22, bf16[8192,128]{1,0:T(8,128)(2,1)} %bitcast.24, bf16[16,2,128,128]{3,2,1,0:T(8,128)(2,1)} %bitcast.31), custom_call_target="tpu_custom_call" | custom-call | tf_op jit(solution)/shard_map/pallas_call | solution.py:117
  165.0 10.3 %fusion.2.t_ref = bf16[1,128,5376]{2,1,0:T(8,128)(2,1)S(1)} fusion(bf16[2048,5376]{1,0:T(8,128)(2,1)} %param.7, bf16[256,2048]{1,0:T(8,128)(2,1)S(1)} %bitcast.27, s32[]{:T(128)S(6)} %select_n.5), kind=kOutput, calls=%fused_computation.4 | convolution fusion | flops 2819260416 | bytes 23920644 | tf_op jit(solution)/shard_map/dot_general | solution.py:345
  175.3 36.5 %shard_map.49 = (bf16[2,128,2048]{2,1,0:T(8,128)(2,1)S(1)}, bf16[1,128,5376]{2,1,0:T(8,128)(2,1)S(1)}) custom-call(bf16[16,2,128,128]{3,2,1,0:T(8,128)(2,1)S(1)} %bitcast.30, bf16[1,128,5376]{2,1,0:T(8,128)(2,1)S(1)} %fusion.2.t_ref), custom_call_target="tpu_custom_call" | custom-call | tf_op jit(solution)/shard_map/pallas_call | solution.py:321
  211.9 0.0 copy-start.6
  211.9 5.4 %fusion.21 = bf16[128,1792]{1,0:T(8,128)(2,1)} fusion(bf16[2048,5376]{1,0:T(8,128)(2,1)} %param.7, bf16[256,2048]{1,0:T(8,128)(2,1)S(1)} %bitcast.33, s32[]{:T(128)S(6)} %select_n.5), kind=kOutput, calls=%fused_computation.20 | convolution fusion | flops 939753472 | bytes 8323076 | tf_op jit(solution)/shard_map/dot_general | solution.py:345
  217.2 0.5 collective-permute-start.2
  217.8 5.0 %fusion.18 = bf16[128,1792]{1,0:T(8,128)(2,1)} fusion(bf16[2048,5376]{1,0:T(8,128)(2,1)} %param.7, bf16[256,2048]{1,0:T(8,128)(2,1)S(1)} %bitcast.34, s32[]{:T(128)S(6)} %select_n.5), kind=kOutput, calls=%fused_computation.19 | convolution fusion | flops 939753472 | bytes 8323076 | tf_op jit(solution)/shard_map/dot_general | solution.py:345
  222.8 1.5 collective-permute-start.1
  224.3 0.0 copy-done.6
  224.3 5.0 %fusion.15 = bf16[128,1792]{1,0:T(8,128)(2,1)} fusion(bf16[2048,5376]{1,0:T(8,128)(2,1)} %param.7, bf16[256,2048]{1,0:T(8,128)(2,1)S(1)} %bitcast.35, s32[]{:T(128)S(6)} %select_n.5), kind=kOutput, calls=%fused_computation.18 | convolution fusion | flops 939753472 | bytes 8323076 | tf_op jit(solution)/shard_map/dot_general | solution.py:345
  229.3 0.5 collective-permute-start
  229.8 0.0 copy-start.7
  229.8 10.4 %fusion.1 = bf16[1,1,128,5376]{3,2,1,0:T(8,128)(2,1)S(1)} fusion(bf16[2048,5376]{1,0:T(8,128)(2,1)} %param.7, bf16[1,128,5376]{2,1,0:T(8,128)(2,1)S(1)} %get-tuple-element.21, bf16[256,2048]{1,0:T(8,128)(2,1)S(1)} %bitcast.28, s32[]{:T(128)S(6)} %select_n.4), kind=kOutput, calls=%fused_computation.3 | convolution fusion | flops 2820636672 | bytes 25296900 | tf_op jit(solution)/shard_map/dot_general | solution.py:345
  240.2 0.0 collective-permute-done.2
  240.2 0.0 copy-done.7
  240.2 4.4 %add_convert_fusion = bf16[128,1792]{1,0:T(8,128)(2,1)S(1)} fusion(bf16[128,1792]{1,0:T(8,128)(2,1)} %collective-permute-done.2, bf16[2048,5376]{1,0:T(8,128)(2,1)} %param.7, bf16[256,2048]{1,0:T(8,128)(2,1)S(1)} %bitcast.36, s32[]{:T(128)S(6)} %select_n.4), kind=kOutput, calls=%fused_computation.22 | convolution fusion | flops 940212224 | bytes 8781828 | tf_op jit(solution)/shard_map/dot_general | solution.py:345
  244.6 0.0 collective-permute-done.1
  244.6 4.2 %add_convert_fusion.1 = bf16[128,1792]{1,0:T(8,128)(2,1)S(1)} fusion(bf16[128,1792]{1,0:T(8,128)(2,1)S(1)} %collective-permute-done.1, bf16[2048,5376]{1,0:T(8,128)(2,1)} %param.7, bf16[256,2048]{1,0:T(8,128)(2,1)S(1)} %bitcast.37, s32[]{:T(128)S(6)} %select_n.4), kind=kOutput, calls=%fused_computation.23 | convolution fusion | flops 940212224 | bytes 8781828 | tf_op jit(solution)/shard_map/dot_general | solution.py:345
  248.8 0.3 collective-permute-done
  249.1 4.2 %add_convert_fusion.2 = bf16[128,1792]{1,0:T(8,128)(2,1)S(1)} fusion(bf16[128,1792]{1,0:T(8,128)(2,1)S(1)} %collective-permute-done, bf16[2048,5376]{1,0:T(8,128)(2,1)} %param.7, bf16[256,2048]{1,0:T(8,128)(2,1)S(1)} %bitcast.38, s32[]{:T(128)S(6)} %select_n.4), kind=kOutput, calls=%fused_computation.24 | convolution fusion | flops 940212224 | bytes 8781828 | tf_op jit(solution)/shard_map/dot_general | solution.py:345
  253.3 0.1 maximum_bitcast_fusion
  253.4 1.8 pad_maximum_fusion
Async XLA Ops:
  0.0 1.6 copy-start.2
  1.6 1.2 copy-start.3
  2.8 1.2 copy-start.4
  62.2 1.3 copy-start
  63.5 1.3 copy-start.1
  126.0 1.0 copy-start.5
  211.9 12.4 %copy-start.6 = (bf16[2,128,2048]{2,1,0:T(8,128)(2,1)}, bf16[2,128,2048]{2,1,0:T(8,128)(2,1)S(1)}, u32[]{:S(2)}) copy-start(bf16[2,128,2048]{2,1,0:T(8,128)(2,1)S(1)} %get-tuple-element.22) | copy-start | bytes 3145732
  217.2 23.0 %collective-permute-start.2 = (bf16[128,1792]{1,0:T(8,128)(2,1)}, bf16[128,1792]{1,0:T(8,128)(2,1)}, u32[]{:S(2)}, u32[]{:S(2)}) collective-permute-start(bf16[128,1792]{1,0:T(8,128)(2,1)} %fusion.21), channel_id=1, source_target_pairs={{0,1},{1,0},{2,3},{3,2},{4,5},{5,4},{6,7},{7,6},{8,9},{9,8},{10,11... | collective-permute-start | bytes 1376264 | tf_op jit(solution)/shard_map/ppermute | solution.py:370
  222.8 21.8 %collective-permute-start.1 = (bf16[128,1792]{1,0:T(8,128)(2,1)}, bf16[128,1792]{1,0:T(8,128)(2,1)S(1)}, u32[]{:S(2)}, u32[]{:S(2)}) collective-permute-start(bf16[128,1792]{1,0:T(8,128)(2,1)} %fusion.18), channel_id=1, source_target_pairs={{0,1},{1,0},{2,3},{3,2},{4,5},{5,4},{6,7},{7,6},{8,9},{9,8},{10,11... | collective-permute-start | bytes 1376264 | tf_op jit(solution)/shard_map/ppermute | solution.py:370
  229.3 19.8 %collective-permute-start = (bf16[128,1792]{1,0:T(8,128)(2,1)}, bf16[128,1792]{1,0:T(8,128)(2,1)S(1)}, u32[]{:S(2)}, u32[]{:S(2)}) collective-permute-start(bf16[128,1792]{1,0:T(8,128)(2,1)} %fusion.15), channel_id=1, source_target_pairs={{0,1},{1,0},{2,3},{3,2},{4,5},{5,4},{6,7},{7,6},{8,9},{9,8},{10,11... | collective-permute-start | bytes 1376264 | tf_op jit(solution)/shard_map/ppermute | solution.py:370
  229.8 10.4 %copy-start.7 = (bf16[2,128,2048]{2,1,0:T(8,128)(2,1)S(1)}, bf16[2,128,2048]{2,1,0:T(8,128)(2,1)}, u32[]{:S(2)}) copy-start(bf16[2,128,2048]{2,1,0:T(8,128)(2,1)} %copy-done.6) | copy-start | bytes 3145732

commit v4 on v3

--- a/solution.py
+++ b/solution.py
@@ -339,23 +339,20 @@
     )(x, terms)
 
 
-def dot_rows(attended, out_weight, dest, columns):
-    rows = attended.shape[0] // lax.axis_size("head")
-    x = lax.dynamic_slice_in_dim(attended, dest * rows, rows, 0)
-    return jnp.dot(x, out_weight[:, columns], preferred_element_type=jnp.float32)
-
-
-def peer_terms(attended, out_weight, columns):
+def product(attended, out_weight, columns):
+    y = jnp.dot(attended, out_weight[:, columns], preferred_element_type=jnp.float32)
+    return lax.optimization_barrier(y.astype(jnp.bfloat16))
+
+
+def rows_for(y, shift):
     heads = lax.axis_size("head")
-    mine = lax.axis_index("head")
-    return [
-        dot_rows(attended, out_weight, lax.rem(mine + k, heads), columns).astype(jnp.bfloat16)
-        for k in range(1, heads)
-    ]
-
-
-def project_end(attended, out_weight, columns, got):
-    total = dot_rows(attended, out_weight, lax.axis_index("head"), columns)
+    rows = y.shape[0] // heads
+    dest = lax.rem(lax.axis_index("head") + shift, heads)
+    return lax.dynamic_slice_in_dim(y, dest * rows, rows, 0)
+
+
+def finish(y, got):
+    total = rows_for(y, 0).astype(jnp.float32)
     for term in got:
         total = total + term.astype(jnp.float32)
     return total.astype(jnp.bfloat16)
@@ -364,16 +361,15 @@
 def project_last(attended, out_weight, chunks):
     heads = lax.axis_size("head")
     step = out_weight.shape[1] // chunks
-    cuts = [slice(c * step, (c + 1) * step) for c in range(chunks)]
+    ys = [product(attended, out_weight, slice(c * step, (c + 1) * step)) for c in range(chunks)]
     received = [
         [
-            lax.ppermute(term, "head", [(i, (i + k) % heads) for i in range(heads)])
-            for k, term in enumerate(peer_terms(attended, out_weight, cut), 1)
+            lax.ppermute(rows_for(y, k), "head", [(i, (i + k) % heads) for i in range(heads)])
+            for k in range(1, heads)
         ]
-        for cut in cuts
+        for y in ys
     ]
-    done = [project_end(attended, out_weight, cut, got) for cut, got in zip(cuts, received)]
-    return jnp.concatenate(done, axis=1)
+    return jnp.concatenate([finish(y, got) for y, got in zip(ys, received)], axis=1)
 
 
 def per_device(queries, key_rows, values, out_weight):
@@ -390,7 +386,7 @@
     ph = run_rows // phases
     lay = (n, parts, runs, run_rows, ph, span)
     columns = out_weight.shape[1]
-    chunks = 3 if columns % (3 * HD) == 0 else 1
+    chunks = 6 if columns % (6 * HD) == 0 else 1
     grid = queries.reshape(groups, run_rows, qh * HD)
     q0, k, v = gather_heads(lay, grid, key_rows, values, n // kvh)
     k = k.reshape(n * span, HD)
@@ -400,11 +396,11 @@
     out0, q1 = attention(lay, 0, "queries", q0.reshape(-1, HD), k, v, grid, own)
     out1, att0 = attention(lay, 1, "heads", q1.reshape(-1, HD), k, v, out0.reshape(own), back)
     att0 = att0.reshape(groups * ph, qh * HD)
-    every = slice(0, columns)
-    terms = jnp.stack(peer_terms(att0, out_weight, every))
+    y0 = product(att0, out_weight, slice(0, columns))
+    terms = jnp.stack([rows_for(y0, k) for k in range(1, heads)])
     att1, got = return_heads(lay, out1.reshape(own), back, terms)
     second = project_last(att1.reshape(groups * ph, qh * HD), out_weight, chunks)
-    first = project_end(att0, out_weight, every, [got[k] for k in range(heads - 1)])
+    first = finish(y0, [got[k] for k in range(heads - 1)])
     ends = [x.reshape(groups // heads, 1, ph, columns) for x in (first, second)]
     return jnp.concatenate(ends, axis=1).reshape(span // heads, columns)
 

time: 256 us -> 261 us (1.020)
  matrix products: 48.8 us -> 34.5 us
  other arithmetic: 1.86 us -> 8.53 us
  local copies, waits for them, and re-layouts: 7.66 us -> 13 us
  waiting for transfers between devices: 0.26 us -> 5.15 us
  starting transfers between devices: 2.56 us -> 5.45 us
    dot_general x8 -> x7, matrix products: 48.8 us -> 34.5 us  [product(): jnp.dot(attended, out_weight[:, columns], preferred_element_type=jnp.floa...]
    ppermute x3 -> x6, waiting for transfers between devices: 0.26 us -> 5.15 us  [project_last(): lax.ppermute(rows_for(y, k), 'head', [(i, (i + k) % heads) for i in range...]
    unnamed x0 -> x5, other arithmetic: none -> 4.1 us
    dynamic_slice x0 -> x6, local copies, waits for them, and re-layouts: none -> 3.79 us  [rows_for(): return lax.dynamic_slice_in_dim(y, dest * rows, rows, 0)]
    ppermute x3 -> x6, starting transfers between devices: 2.56 us -> 5.45 us  [project_last(): lax.ppermute(rows_for(y, k), 'head', [(i, (i + k) % heads) for i in range...]
    unnamed x16 -> x24, local copies, waits for them, and re-layouts: 7.66 us -> 7.74 us
  transfers between devices with their start and end apart: 3 -> 6, of which waited for: 1 -> 2; matrix products, arithmetic and copies ran while one was open for 11% -> 10% of each run, Pallas kernels for 0% -> 0%
where the time goes in v4:
time: 261 us; the launch traced here: 260 us
  Pallas kernels  194 us (74%)
  matrix products  34.5 us (13%)
  local copies, waits for them, and re-layouts  13 us (5%)
  other arithmetic  8.53 us (3%)
  starting transfers between devices  5.45 us (2%)
  waiting for transfers between devices  5.15 us (2%)
    pallas_call x2, Pallas kernels, attention(): pl.pallas_call(functools.partial(attn_kernel, lay, phase, carry), in_spec...  99.1 us
    pallas_call x1, Pallas kernels, gather_heads(): pl.pallas_call(functools.partial(inbound, lay, dup), in_specs=[any_space]...  58.1 us
    pallas_call x1, Pallas kernels, return_heads(): pl.pallas_call(functools.partial(outbound, lay, heads), in_specs=[space,...  36.5 us
    dot_general x7, matrix products, product(): jnp.dot(attended, out_weight[:, columns], preferred_element_type=jnp.floa...  34.5 us
    unnamed x24, local copies, waits for them, and re-layouts  7.74 us
    ppermute x6, starting transfers between devices, project_last(): lax.ppermute(rows_for(y, k), 'head', [(i, (i + k) % heads) for i in range...  5.45 us
  transfers between devices with their start and end apart: 6, of which 2 were waited for; matrix products, arithmetic and copies ran while one was open for 10% of the time, Pallas kernels for 0%

profile of v4, /device:TPU:0, one launch (start us, length us, event | category | flops | bytes accessed | tf_op | source)
XLA Modules:
  0.0 260.4 jit_solution(5048246786619517661)
XLA Ops:
  0.0 0.0 copy-start.2
  0.0 1.6 copy-done.2
  1.6 0.0 copy-start.3
  1.6 1.2 copy-done.3
  2.8 0.0 copy-start.4
  2.8 1.2 copy-done.4
  4.0 58.1 %shard_map.46 = (bf16[16,2,128,128]{3,2,1,0:T(8,128)(2,1)S(1)}, bf16[16,512,128]{2,1,0:T(8,128)(2,1)S(1)}, bf16[16,512,128]{2,1,0:T(8,128)(2,1)S(1)}) custom-call(bf16[2,256,2048]{2,1,0:T(8,128)(2,1)S(1)} %bitcast.31, bf16[512,1024]{1,0:T(8,128)(2,1)S(1)} %copy-done.3, bf16[512,1024]{1,0:T(8,128)(2,1)S(1)} %copy-done.4), custom_call_target="tpu_custom_call" | custom-call | tf_op jit(solution)/shard_map/pallas_call | solution.py:245
  62.2 0.0 copy-start
  62.2 1.3 copy-done
  63.5 0.0 copy-start.1
  63.5 1.3 copy-done.1
  64.8 61.2 %shard_map.47 = (bf16[4096,128]{1,0:T(8,128)(2,1)S(1)}, bf16[16,2,128,128]{3,2,1,0:T(8,128)(2,1)S(1)}) custom-call(bf16[4096,128]{1,0:T(8,128)(2,1)S(1)} %bitcast.32, bf16[8192,128]{1,0:T(8,128)(2,1)} %bitcast.26, bf16[8192,128]{1,0:T(8,128)(2,1)} %bitcast.28, bf16[2,256,2048]{2,1,0:T(8,128)(2,1)} %bitcast.30), custom_call_target="tpu_custom_call" | custom-call | tf_op jit(solution)/shard_map/pallas_call | solution.py:117
  126.0 0.0 copy-start.5
  126.0 1.0 copy-done.5
  127.0 37.9 %shard_map.48 = (bf16[4096,128]{1,0:T(8,128)(2,1)S(1)}, bf16[2,128,2048]{2,1,0:T(8,128)(2,1)S(1)}) custom-call(bf16[4096,128]{1,0:T(8,128)(2,1)S(1)} %bitcast.35, bf16[8192,128]{1,0:T(8,128)(2,1)} %bitcast.27, bf16[8192,128]{1,0:T(8,128)(2,1)} %bitcast.29, bf16[16,2,128,128]{3,2,1,0:T(8,128)(2,1)} %bitcast.34), custom_call_target="tpu_custom_call" | custom-call | tf_op jit(solution)/shard_map/pallas_call | solution.py:117
  164.9 14.6 %convolution_convert_fusion = bf16[256,5376]{1,0:T(8,128)(2,1)} fusion(bf16[256,2048]{1,0:T(8,128)(2,1)S(1)} %bitcast.42, bf16[2048,5376]{1,0:T(8,128)(2,1)} %param.7), kind=kOutput, calls=%fused_computation | convolution fusion | flops 5638520832 | bytes 25821184 | tf_op jit(solution)/shard_map/dot_general | solution.py:343
  179.5 1.4 dynamic-slice_bitcast_fusion.t_ref
  180.9 36.5 %shard_map.49 = (bf16[2,128,2048]{2,1,0:T(8,128)(2,1)S(1)}, bf16[1,128,5376]{2,1,0:T(8,128)(2,1)S(1)}) custom-call(bf16[16,2,128,128]{3,2,1,0:T(8,128)(2,1)S(1)} %bitcast.33, bf16[1,128,5376]{2,1,0:T(8,128)(2,1)S(1)} %dynamic-slice_bitcast_fusion.t_ref), custom_call_target="tpu_custom_call" | custom-call | tf_op jit(solution)/shard_map/pallas_call | solution.py:321
  217.4 3.3 %fusion.29 = bf16[256,896]{1,0:T(8,128)(2,1)S(1)} fusion(bf16[256,2048]{1,0:T(8,128)(2,1)S(1)} %bitcast.36, bf16[2048,5376]{1,0:T(8,128)(2,1)} %param.7), kind=kOutput, calls=%fused_computation.23 | convolution fusion | flops 939753472 | bytes 5177344 | tf_op jit(solution)/shard_map/dot_general | solution.py:343
  220.7 0.7 constant_dynamic-slice_fusion
  221.4 0.5 collective-permute-start.5
  222.0 3.3 %fusion.26 = bf16[256,896]{1,0:T(8,128)(2,1)S(1)} fusion(bf16[256,2048]{1,0:T(8,128)(2,1)S(1)} %bitcast.37, bf16[2048,5376]{1,0:T(8,128)(2,1)} %param.7), kind=kOutput, calls=%fused_computation.22 | convolution fusion | flops 939753472 | bytes 5177344 | tf_op jit(solution)/shard_map/dot_general | solution.py:343
  225.3 0.7 constant_dynamic-slice_fusion.1
  226.0 1.5 collective-permute-start.4
  227.5 3.3 %fusion.23 = bf16[256,896]{1,0:T(8,128)(2,1)S(1)} fusion(bf16[256,2048]{1,0:T(8,128)(2,1)S(1)} %bitcast.38, bf16[2048,5376]{1,0:T(8,128)(2,1)} %param.7), kind=kOutput, calls=%fused_computation.21 | convolution fusion | flops 939753472 | bytes 5177344 | tf_op jit(solution)/shard_map/dot_general | solution.py:343
  230.8 0.0 copy-start.6
  230.8 0.8 constant_dynamic-slice_fusion.2
  231.6 0.5 collective-permute-start.3
  232.1 3.3 %fusion.20 = bf16[256,896]{1,0:T(8,128)(2,1)S(1)} fusion(bf16[256,2048]{1,0:T(8,128)(2,1)S(1)} %bitcast.39, bf16[2048,5376]{1,0:T(8,128)(2,1)} %param.7), kind=kOutput, calls=%fused_computation.20 | convolution fusion | flops 939753472 | bytes 5177344 | tf_op jit(solution)/shard_map/dot_general | solution.py:343
  235.4 0.0 copy-done.6
  235.4 0.0 copy-start.8
  235.4 0.8 constant_dynamic-slice_fusion.3
  236.2 1.5 collective-permute-start.2
  237.7 3.3 %fusion.14 = bf16[256,896]{1,0:T(8,128)(2,1)S(1)} fusion(bf16[256,2048]{1,0:T(8,128)(2,1)S(1)} %bitcast.40, bf16[2048,5376]{1,0:T(8,128)(2,1)} %param.7), kind=kOutput, calls=%fused_computation.18 | convolution fusion | flops 939753472 | bytes 5177344 | tf_op jit(solution)/shard_map/dot_general | solution.py:343
  241.0 0.0 copy-done.8
  241.0 0.0 copy-start.10
  241.0 0.8 constant_dynamic-slice_fusion.5
  241.8 0.1 copy-done.10
  241.8 0.5 collective-permute-start
  242.4 1.7 fusion.13
  244.0 0.0 copy-start.11
  244.0 0.0 copy-start.9
  244.0 0.0 copy-start.7
  244.0 3.4 %fusion.17 = bf16[256,896]{1,0:T(8,128)(2,1)S(1)} fusion(bf16[256,2048]{1,0:T(8,128)(2,1)S(1)} %bitcast.41, bf16[2048,5376]{1,0:T(8,128)(2,1)} %param.7), kind=kOutput, calls=%fused_computation.19 | convolution fusion | flops 939753472 | bytes 5177344 | tf_op jit(solution)/shard_map/dot_general | solution.py:343
  247.5 1.0 collective-permute-done
  248.5 0.9 collective-permute-start.1
  249.3 0.0 copy-done.11
  249.3 1.0 fusion.32
  250.3 4.2 %collective-permute-done.1 = bf16[128,896]{1,0:T(8,128)(2,1)S(1)} collective-permute-done((bf16[128,896]{1,0:T(8,128)(2,1)S(1)}, bf16[128,896]{1,0:T(8,128)(2,1)S(1)}, u32[]{:S(2)}, u32[]{:S(2)}) %collective-permute-start.1) | collective-permute-done | bytes 229408 | tf_op jit(solution)/shard_map/ppermute | solution.py:367
  254.5 0.1 fusion.33
  254.6 0.0 collective-permute-done.2
  254.6 0.0 copy-done.9
  254.6 1.0 fusion.34
  255.6 0.0 collective-permute-done.3
  255.6 0.0 copy-done.7
  255.6 1.0 fusion.35
  256.6 0.0 collective-permute-done.4
  256.6 1.0 fusion.36
  257.6 0.0 collective-permute-done.5
  257.6 1.0 fusion.37
  258.7 1.8 pad_maximum_fusion
  (1 shorter events, 0.0 us)
Async XLA Ops:
  0.0 1.6 copy-start.2
  1.6 1.2 copy-start.3
  2.8 1.2 copy-start.4
  62.2 1.3 copy-start
  63.5 1.3 copy-start.1
  126.0 1.0 copy-start.5
  221.4 36.2 %collective-permute-start.5 = (bf16[128,896]{1,0:T(8,128)(2,1)}, bf16[128,896]{1,0:T(8,128)(2,1)}, u32[]{:S(2)}, u32[]{:S(2)}) collective-permute-start(bf16[128,896]{1,0:T(8,128)(2,1)} %constant_dynamic-slice_fusion), channel_id=1, source_target_pairs={{0,1},{1,0},{2,3},{3,2},{4,5},{5,4},{6,7},{7,6},{8,9},{9,8},{10,11... | collective-permute-start | bytes 688136 | tf_op jit(solution)/shard_map/ppermute | solution.py:367
  226.0 30.6 %collective-permute-start.4 = (bf16[128,896]{1,0:T(8,128)(2,1)}, bf16[128,896]{1,0:T(8,128)(2,1)}, u32[]{:S(2)}, u32[]{:S(2)}) collective-permute-start(bf16[128,896]{1,0:T(8,128)(2,1)} %constant_dynamic-slice_fusion.1), channel_id=1, source_target_pairs={{0,1},{1,0},{2,3},{3,2},{4,5},{5,4},{6,7},{7,6},{8,9},{9,8},{10,11... | collective-permute-start | bytes 688136 | tf_op jit(solution)/shard_map/ppermute | solution.py:367
  230.8 4.6 %copy-start.6 = (bf16[256,896]{1,0:T(8,128)(2,1)}, bf16[256,896]{1,0:T(8,128)(2,1)S(1)}, u32[]{:S(2)}) copy-start(bf16[256,896]{1,0:T(8,128)(2,1)S(1)} %fusion.23) | copy-start | bytes 1376260
  231.6 24.0 %collective-permute-start.3 = (bf16[128,896]{1,0:T(8,128)(2,1)}, bf16[128,896]{1,0:T(8,128)(2,1)}, u32[]{:S(2)}, u32[]{:S(2)}) collective-permute-start(bf16[128,896]{1,0:T(8,128)(2,1)} %constant_dynamic-slice_fusion.2), channel_id=1, source_target_pairs={{0,1},{1,0},{2,3},{3,2},{4,5},{5,4},{6,7},{7,6},{8,9},{9,8},{10,11... | collective-permute-start | bytes 688136 | tf_op jit(solution)/shard_map/ppermute | solution.py:367
  235.4 5.6 %copy-start.8 = (bf16[256,896]{1,0:T(8,128)(2,1)}, bf16[256,896]{1,0:T(8,128)(2,1)S(1)}, u32[]{:S(2)}) copy-start(bf16[256,896]{1,0:T(8,128)(2,1)S(1)} %fusion.20) | copy-start | bytes 1376260
  236.2 18.4 %collective-permute-start.2 = (bf16[128,896]{1,0:T(8,128)(2,1)}, bf16[128,896]{1,0:T(8,128)(2,1)}, u32[]{:S(2)}, u32[]{:S(2)}) collective-permute-start(bf16[128,896]{1,0:T(8,128)(2,1)} %constant_dynamic-slice_fusion.3), channel_id=1, source_target_pairs={{0,1},{1,0},{2,3},{3,2},{4,5},{5,4},{6,7},{7,6},{8,9},{9,8},{10,11... | collective-permute-start | bytes 688136 | tf_op jit(solution)/shard_map/ppermute | solution.py:367
  241.0 0.8 copy-start.10
  241.8 6.6 %collective-permute-start = (bf16[128,896]{1,0:T(8,128)(2,1)}, bf16[128,896]{1,0:T(8,128)(2,1)}, u32[]{:S(2)}, u32[]{:S(2)}) collective-permute-start(bf16[128,896]{1,0:T(8,128)(2,1)} %constant_dynamic-slice_fusion.5), channel_id=1, source_target_pairs={{0,1},{1,0},{2,3},{3,2},{4,5},{5,4},{6,7},{7,6},{8,9},{9,8},{10,11... | collective-permute-start | bytes 688136 | tf_op jit(solution)/shard_map/ppermute | solution.py:367
  244.0 5.3 %copy-start.11 = (bf16[256,896]{1,0:T(8,128)(2,1)S(1)}, bf16[256,896]{1,0:T(8,128)(2,1)}, u32[]{:S(2)}) copy-start(bf16[256,896]{1,0:T(8,128)(2,1)} %copy-done.10) | copy-start | bytes 1376260
  244.0 10.5 %copy-start.9 = (bf16[256,896]{1,0:T(8,128)(2,1)S(1)}, bf16[256,896]{1,0:T(8,128)(2,1)}, u32[]{:S(2)}) copy-start(bf16[256,896]{1,0:T(8,128)(2,1)} %copy-done.8) | copy-start | bytes 1376260
  244.0 11.6 %copy-start.7 = (bf16[256,896]{1,0:T(8,128)(2,1)S(1)}, bf16[256,896]{1,0:T(8,128)(2,1)}, u32[]{:S(2)}) copy-start(bf16[256,896]{1,0:T(8,128)(2,1)} %copy-done.6) | copy-start | bytes 1376260
  248.5 6.0 %collective-permute-start.1 = (bf16[128,896]{1,0:T(8,128)(2,1)S(1)}, bf16[128,896]{1,0:T(8,128)(2,1)S(1)}, u32[]{:S(2)}, u32[]{:S(2)}) collective-permute-start(bf16[128,896]{1,0:T(8,128)(2,1)S(1)} %constant_dynamic-slice_fusion.4), channel_id=1, source_target_pairs={{0,1},{1,0},{2,3},{3,2},{4,5},{5,4},{6,7},{7,6},{8,9},{9,8},{10,11... | collective-permute-start | bytes 688136 | tf_op jit(solution)/shard_map/ppermute | solution.py:367
